TPU v7x, 32 devices: a whole 2x2x4 slice. The times are simulated.
32 devices in a mesh: parts: 2 (over x), rows: 16 (over z, y, core).
Axes of the slice: x: 2, y: 2, z: 4, core: 2. Of those that a mesh axis runs over, the one named last changes fastest.
Arguments:
- rhs: float32 [3, 12288, 256], P(None, 'rows', 'parts'), parts along dimension 2, may hold values from -6 to 6
- diag_inv: float32 [3, 12288, 768], P(None, 'rows'), may hold values from -0.21875 to 0.21875
- tiles: float32 [2, 32, 768, 768], P(None, 'rows'), may hold values from -0.15625 to 0.15625
- dest: int32 [2, 16, 2], P(None, 'rows'), may hold values from 0 to 15, all different within a row; in each aligned block of 16 rows (0 to 15, 16 to 31, ..., all dimensions but the last counted through in order) at most 4 rows name the same one
- obs_weight: float32 [12288], P('rows'), may hold values from -0.108253175 to 0.108253175, as said below
Outputs:
- solution: float32 [3, 12288, 256], P(None, 'rows', 'parts'), parts along dimension 2
- observed: float32 [256], P('parts'), parts along dimension 0
There are 2 independent parts, one for each index of `parts`. A program takes and returns all parts, laid end to end along the dimension named above; an argument that names none is the same for every part. Nothing has to cross between parts.
Inputs may be any that keep to these rules, and one draw needn't show every extreme that they name: `dest`: in each of the two levels, the two entries of a supernode differ, and no supernode of the next level is named more than 4 times. `obs_weight`: finite weights.
All inputs are finite; a program needn't handle non-finite values.
Results may differ from a plain program's by a relative error of at most 0.00029.
Values sent between devices are 32-bit elements; how exact they have to be, the bound alone decides.
No kernel may reach another device: no remote copies, remote signals or barrier semaphores. Data moves between devices by JAX's collectives and lax.ppermute only.
A program may use at most 128 MiB of HBM per device.

v0:
```python
import jax
import jax.numpy as jnp
from jax import lax
from jax.sharding import PartitionSpec as P


def collect_updates(solved_block, tiles_level, pattern_level):
    products = jnp.einsum(
        "kab,bc->kac",
        tiles_level,
        solved_block,
        precision=lax.Precision.HIGHEST,
        preferred_element_type=jnp.float32,
    )
    block_rows = solved_block.shape[0]
    width = products.shape[2]
    count = lax.axis_size("rows")
    sliced = lax.all_to_all(products, "rows", split_axis=1, concat_axis=0, tiled=True)
    owners = jnp.arange(count, dtype=jnp.int32)
    flat_targets = pattern_level.reshape(-1)
    matches = (owners[:, None] == flat_targets[None, :]).astype(jnp.float32)
    partial_value = jnp.einsum("mq,qac->mac", matches, sliced, precision=lax.Precision.HIGHEST)
    returned = lax.all_to_all(partial_value, "rows", split_axis=0, concat_axis=0, tiled=True)
    return returned.reshape(block_rows, width)


def body(rhs, diag_inv, tiles, dest, obs_weight):
    pattern = lax.all_gather(dest, "rows", axis=1, tiled=True)
    current = rhs[0]
    solved_levels = []
    solved_block = current
    for section in range(3):
        solved_block = jnp.dot(
            diag_inv[section],
            current,
            precision=lax.Precision.HIGHEST,
            preferred_element_type=jnp.float32,
        )
        solved_levels.append(solved_block)
        if section < 2:
            current = rhs[section + 1] - collect_updates(
                solved_block, tiles[section], pattern[section]
            )
    partial_sum = jnp.dot(
        obs_weight,
        solved_block,
        precision=lax.Precision.HIGHEST,
        preferred_element_type=jnp.float32,
    )
    observed = lax.psum(partial_sum, "rows")
    return (jnp.stack(solved_levels), observed)


def solution(mesh):
    in_specs = (
        P(None, "rows", "parts"),
        P(None, "rows", None),
        P(None, "rows", None, None),
        P(None, "rows", None),
        P("rows"),
    )
    out_specs = (P(None, "rows", "parts"), P("parts"))
    return jax.shard_map(body, mesh=mesh, in_specs=in_specs, out_specs=out_specs, check_vma=False)
```

profile of v0, /device:TPU:0, one launch (start us, length us, event | category | flops | bytes accessed | tf_op | source)
XLA Modules:
  0.0 156.5 jit_solution(14306570408259959369)
XLA Ops:
  0.6 3.7 %fusion.10 = f32[768,128]{1,0:T(8,128)S(1)} fusion(f32[3,768,768]{2,1,0:T(8,128)} %param.6, f32[3,768,128]{2,1,0:T(8,128)} %param.5), kind=kOutput, calls=%fused_computation.10 | convolution fusion | flops 905969664 | bytes 3145728 | tf_op jit(solution)/shard_map/dot_general | solution.py:33
  4.3 7.4 %fusion.15 = f32[2,768,128]{1,2,0:T(8,128)S(1)} fusion(f32[2,2,768,768]{3,2,1,0:T(8,128)} %param.7, f32[768,128]{1,0:T(8,128)S(1)} %fusion.10), kind=kOutput, calls=%fused_computation.15 | convolution fusion | flops 1811939328 | bytes 5898240 | tf_op jit(solution)/shard_map/kab,bc->kac/dot_general | solution.py:8
  11.7 0.0 copy-start.3
  11.7 1.2 copy.23
  12.9 7.5 %all-to-all-start = ((f32[2,768,128]{2,0,1:T(2,128)}), f32[2,768,128]{2,0,1:T(2,128)S(1)}, u32[]{:S(2)}, u32[]{:S(2)}) async-start(f32[2,768,128]{2,0,1:T(2,128)} %copy.23), calls=%async_computation | async-start | bytes 1572864 | tf_op jit(solution)/shard_map/all_to_all | solution.py:18
  20.4 29.2 %all_gather.3 = s32[2,16,2]{2,0,1:T(2,128)S(1)} all-gather(s32[2,1,2]{2,0,1:T(2,128)S(1)} %bitcast.82), channel_id=1, replica_groups=mesh['parts'=2,'rows'=16] {'rows'}, dimensions={1}, use_global_device_ids=true | all-gather | bytes 272 | tf_op jit(solution)/shard_map/all_gather | solution.py:28
  49.7 0.1 eq.31
  49.8 0.0 copy-start
  49.8 0.1 copy.24
  49.8 0.6 copy.25
  50.5 0.4 fusion.29
  50.8 0.1 copy.26
  51.0 16.7 %all_to_all.46 = f32[16,48,128]{2,1,0:T(8,128)S(1)} all-to-all(f32[16,48,128]{2,1,0:T(8,128)S(1)} %copy.26), channel_id=1, replica_groups=mesh['parts'=2,'rows'=16] {'rows'}, dimensions={0} | all-to-all | bytes 786432 | tf_op jit(solution)/shard_map/all_to_all | solution.py:23
  67.7 0.1 bitcast_subtract_fusion.1
  67.8 3.8 %fusion.8 = f32[128,768]{1,0:T(8,128)S(1)} fusion(f32[3,768,768]{2,1,0:T(8,128)} %param.6, f32[1,768,128]{2,1,0:T(8,128)S(1)} %bitcast_subtract_fusion.1), kind=kOutput, calls=%fused_computation.8 | convolution fusion | flops 905969664 | bytes 3145728 | tf_op jit(solution)/shard_map/dot_general | solution.py:33
  71.5 5.0 %fusion.18 = f32[2,768,128]{1,2,0:T(8,128)S(1)} fusion(f32[2,2,768,768]{3,2,1,0:T(8,128)S(1)} %copy-done, f32[128,768]{1,0:T(8,128)S(1)} %fusion.8), kind=kOutput, calls=%fused_computation.16 | convolution fusion | flops 1811939328 | bytes 5898240 | tf_op jit(solution)/shard_map/kab,bc->kac/dot_general | solution.py:8
  76.5 1.2 copy.28
  77.7 3.6 %all-to-all-start.2 = ((f32[2,768,128]{2,0,1:T(2,128)}), f32[2,768,128]{2,0,1:T(2,128)S(1)}, u32[]{:S(2)}, u32[]{:S(2)}) async-start(f32[2,768,128]{2,0,1:T(2,128)} %copy.28), calls=%async_computation.2 | async-start | bytes 1572864 | tf_op jit(solution)/shard_map/all_to_all | solution.py:18
  81.3 0.1 eq.35
  81.4 18.6 %all-to-all-done.2 = f32[2,768,128]{2,0,1:T(2,128)S(1)} async-done(((f32[2,768,128]{2,0,1:T(2,128)}), f32[2,768,128]{2,0,1:T(2,128)S(1)}, u32[]{:S(2)}, u32[]{:S(2)}) %all-to-all-start.2) | async-done | bytes 786464 | tf_op jit(solution)/shard_map/all_to_all | solution.py:18
  99.9 0.1 copy.29
  100.0 0.0 copy-start.2
  100.0 0.6 copy.30
  100.6 0.4 fusion.32
  101.0 0.9 copy.31
  101.9 5.3 %all-to-all-start.3 = ((f32[16,48,128]{2,1,0:T(8,128)}), f32[16,48,128]{2,1,0:T(8,128)S(1)}, u32[]{:S(2)}, u32[]{:S(2)}) async-start(f32[16,48,128]{2,1,0:T(8,128)} %copy.31), calls=%async_computation.3 | async-start | bytes 786432 | tf_op jit(solution)/shard_map/all_to_all | solution.py:23
  107.3 0.2 copy.27
  107.4 12.0 %all-to-all-done.3 = f32[16,48,128]{2,1,0:T(8,128)S(1)} async-done(((f32[16,48,128]{2,1,0:T(8,128)}), f32[16,48,128]{2,1,0:T(8,128)S(1)}, u32[]{:S(2)}, u32[]{:S(2)}) %all-to-all-start.3) | async-done | bytes 393248 | tf_op jit(solution)/shard_map/all_to_all | solution.py:23
  119.4 3.7 %fusion.6 = f32[128,768]{0,1:T(8,128)S(1)} fusion(f32[3,768,768]{2,1,0:T(8,128)} %param.6, f32[1,768,128]{2,1,0:T(8,128)S(1)} %bitcast_subtract_fusion), kind=kOutput, calls=%fused_computation.6 | convolution fusion | flops 905969664 | bytes 3145728 | tf_op jit(solution)/shard_map/dot_general | solution.py:33
  123.1 0.3 convolution_bitcast_fusion
  123.4 32.0 %psum.7 = f32[128]{0:T(128)} all-reduce(f32[128]{0:T(128)S(1)} %convolution_bitcast_fusion), channel_id=1, replica_groups=mesh['parts'=2,'rows'=16] {'rows'}, use_global_device_ids=true, to_apply=%region_0.0 | all-reduce | flops 128 | bytes 1024 | tf_op jit(solution)/shard_map/psum | solution.py:50
  155.4 1.1 pad_maximum_fusion
  (9 shorter events, 0.1 us)
Async XLA Ops:
  11.7 8.7 %copy-start.3 = (s32[2,1,2]{2,1,0:T(1,128)S(1)}, s32[2,1,2]{2,1,0:T(1,128)}, u32[]{:S(2)}) copy-start(s32[2,1,2]{2,1,0:T(1,128)} %param.8) | copy-start | bytes 52
  12.9 54.8 %copy-start.1 = (f32[3,768,128]{2,1,0:T(8,128)S(1)}, f32[3,768,128]{2,1,0:T(8,128)}, u32[]{:S(2)}) copy-start(f32[3,768,128]{2,1,0:T(8,128)} %param.5) | copy-start | bytes 3538948
  12.9 36.9 %all-to-all-start = ((f32[2,768,128]{2,0,1:T(2,128)}), f32[2,768,128]{2,0,1:T(2,128)S(1)}, u32[]{:S(2)}, u32[]{:S(2)}) async-start(f32[2,768,128]{2,0,1:T(2,128)} %copy.23), calls=%async_computation | async-start | bytes 1572864 | tf_op jit(solution)/shard_map/all_to_all | solution.py:18
  49.8 21.8 %copy-start = (f32[2,2,768,768]{3,2,1,0:T(8,128)S(1)}, f32[2,2,768,768]{3,2,1,0:T(8,128)}, u32[]{:S(2)}) copy-start(f32[2,2,768,768]{3,2,1,0:T(8,128)} %param.7) | copy-start | bytes 28311556
  77.7 22.3 %all-to-all-start.2 = ((f32[2,768,128]{2,0,1:T(2,128)}), f32[2,768,128]{2,0,1:T(2,128)S(1)}, u32[]{:S(2)}, u32[]{:S(2)}) async-start(f32[2,768,128]{2,0,1:T(2,128)} %copy.28), calls=%async_computation.2 | async-start | bytes 1572864 | tf_op jit(solution)/shard_map/all_to_all | solution.py:18
  100.0 7.2 %copy-start.2 = (f32[768]{0:T(1024)S(1)}, f32[768]{0:T(1024)}, u32[]{:S(2)}) copy-start(f32[768]{0:T(1024)} %param.9) | copy-start | bytes 9220
  101.9 17.5 %all-to-all-start.3 = ((f32[16,48,128]{2,1,0:T(8,128)}), f32[16,48,128]{2,1,0:T(8,128)S(1)}, u32[]{:S(2)}, u32[]{:S(2)}) async-start(f32[16,48,128]{2,1,0:T(8,128)} %copy.31), calls=%async_computation.3 | async-start | bytes 786432 | tf_op jit(solution)/shard_map/all_to_all | solution.py:23
where the time goes:
time: 157 us
  blocking collectives  77.9 us (50%)
  waiting for transfers between devices  30.5 us (19%)
  matrix products  24.5 us (16%)
  starting transfers between devices  16.5 us (11%)
  local copies, waits for them, and re-layouts  5.05 us (3%)
    psum x1, blocking collectives, body(): observed = lax.psum(partial_sum, 'rows')  32 us
    all_gather x1, blocking collectives, body(): pattern = lax.all_gather(dest, 'rows', axis=1, tiled=True)  29.2 us
    all_to_all x2, waiting for transfers between devices, collect_updates(): lax.all_to_all(products, 'rows', split_axis=1, concat_axis=0, tiled=True)  18.6 us
    all_to_all x1, blocking collectives, collect_updates(): lax.all_to_all(partial_value, 'rows', split_axis=0, concat_axis=0, tiled=...  16.7 us
    dot_general x2, matrix products, collect_updates(): jnp.einsum('kab,bc->kac', tiles_level, solved_block, precision=lax.Precis...  12.3 us
    all_to_all x1, waiting for transfers between devices, collect_updates(): lax.all_to_all(partial_value, 'rows', split_axis=0, concat_axis=0, tiled=...  12 us
    all_to_all x2, starting transfers between devices, collect_updates(): lax.all_to_all(products, 'rows', split_axis=1, concat_axis=0, tiled=True)  11.2 us
    dot_general x3, matrix products, body(): jnp.dot(diag_inv[section], current, precision=lax.Precision.HIGHEST, pref...  11.1 us
  transfers between devices with their start and end apart: 3, of which 2 were waited for; matrix products, arithmetic and copies ran while one was open for 0% of the time, Pallas kernels for 0%

commit v1 on v0

v1 whole, which is shorter than its diff:
```python
import functools

import jax
import jax.numpy as jnp
from jax import lax
from jax.experimental import pallas as pl
from jax.experimental.pallas import tpu as pltpu
from jax.sharding import PartitionSpec as P

LANES = 128
SUB = 8
ANY = pl.BlockSpec(memory_space=pl.ANY)
VMEM = pl.BlockSpec(memory_space=pltpu.VMEM)
SMEM = pl.BlockSpec(memory_space=pltpu.SMEM)


def split(x):
    hi = x.astype(jnp.bfloat16)
    lo = (x - hi.astype(jnp.float32)).astype(jnp.bfloat16)
    return hi, lo


def split_cols(x):
    hi, lo = split(x)
    return jnp.concatenate([hi, lo], axis=1)


def dot3(a, both):
    width = both.shape[1] // 2
    hi, lo = split(a)
    wide = jnp.dot(hi, both, preferred_element_type=jnp.float32)
    narrow = jnp.dot(lo, both[:, :width], preferred_element_type=jnp.float32)
    return wide[:, :width] + (wide[:, width:] + narrow)


def left_product(vector, matrix, rows):
    columns = vector.T
    total = None
    for r in range(rows // LANES):
        block = matrix[pl.ds(r * LANES, LANES), :]
        term = jnp.sum(columns[:, r : r + 1] * block, axis=0, keepdims=True)
        total = term if total is None else total + term
    return total


def chunked(ref, buf, sem, parts):
    size = buf.shape[0] // parts
    copies = []
    for c in range(parts):
        at = pl.ds(c * size, size)
        copies.append(pltpu.make_async_copy(ref.at[at], buf.at[at], sem.at[c]))
    return copies


def products(tile_bufs, copies, both, pay_ref, group, parts):
    rows = tile_bufs[0].shape[0]
    seg = rows // group
    size = rows // parts
    for k, buf in enumerate(tile_bufs):
        for c in range(parts):
            copies[k][c].wait()
            out = dot3(buf[pl.ds(c * size, size), :], both)
            for s in range(size // seg):
                pay_ref[c * (size // seg) + s, pl.ds(k * seg, seg), :] = out[
                    s * seg : (s + 1) * seg
                ]


def first_kernel(
    group, parts, rhs, diag, tiles, weight, dest, sol, pay,
    b_buf, d_buf, l0_buf, l1_buf, v_buf, y_buf, small, d_sem, l0_sem, l1_sem, v_sem,
):
    rows = b_buf.shape[0]
    seg = rows // group
    d_copies = chunked(diag.at[0], d_buf, d_sem, parts)
    l_copies = [
        chunked(tiles.at[0, 0], l0_buf, l0_sem, parts),
        chunked(tiles.at[0, 1], l1_buf, l1_sem, parts),
    ]
    v_copies = chunked(diag.at[2], v_buf, v_sem, parts)
    b_copy = pltpu.make_async_copy(rhs.at[0], b_buf, small.at[0])
    b_copy.start()
    for copies in (d_copies, *l_copies, v_copies):
        for copy in copies:
            copy.start()
    b_copy.wait()
    both = split_cols(b_buf[...])
    size = rows // parts
    for c in range(parts):
        d_copies[c].wait()
        y_buf[pl.ds(c * size, size), :] = dot3(d_buf[pl.ds(c * size, size), :], both)
    y_copy = pltpu.make_async_copy(y_buf, sol.at[0], small.at[1])
    y_copy.start()
    products([l0_buf, l1_buf], l_copies, split_cols(y_buf[...]), pay, group, parts)
    for copy in v_copies:
        copy.wait()
    vector = left_product(weight[...], v_buf, rows)
    base = 2 * seg
    extra = pay.shape[1] - base
    lines = [jnp.full((1, LANES), dest[0, 0, k].astype(jnp.float32)) for k in range(2)]
    lines += [vector[:, r * LANES : (r + 1) * LANES] for r in range(rows // LANES)]
    if extra > len(lines):
        lines.append(jnp.zeros((extra - len(lines), LANES), jnp.float32))
    meta = jnp.concatenate(lines, axis=0)
    for s in range(group):
        pay[s, pl.ds(base, extra), :] = meta
    y_copy.wait()


def middle_kernel(
    group, parts, sol_in, arrived, rhs, diag, tiles, share, u_vec, dest, sol, pay,
    b_buf, d_buf, l0_buf, l1_buf, y_buf, small, d_sem, l0_sem, l1_sem,
):
    rows = b_buf.shape[0]
    seg = rows // group
    d_copies = chunked(diag.at[1], d_buf, d_sem, parts)
    l_copies = [
        chunked(tiles.at[1, 0], l0_buf, l0_sem, parts),
        chunked(tiles.at[1, 1], l1_buf, l1_sem, parts),
    ]
    b_copy = pltpu.make_async_copy(rhs.at[1], b_buf, small.at[0])
    b_copy.start()
    for copies in (d_copies, *l_copies):
        for copy in copies:
            copy.start()
    b_copy.wait()
    both = split_cols(b_buf[...] - (arrived[0] + arrived[1]))
    size = rows // parts
    for c in range(parts):
        d_copies[c].wait()
        y_buf[pl.ds(c * size, size), :] = dot3(d_buf[pl.ds(c * size, size), :], both)
    y_copy = pltpu.make_async_copy(y_buf, sol.at[1], small.at[1])
    y_copy.start()
    products([l0_buf, l1_buf], l_copies, split_cols(y_buf[...]), pay, group, parts)
    part = share[0:1, :] - left_product(u_vec[...], y_buf, rows)
    base = 2 * seg
    extra = pay.shape[1] - base
    lines = [jnp.full((1, LANES), dest[1, 0, k].astype(jnp.float32)) for k in range(2)]
    lines += [part, jnp.zeros((extra - 3, LANES), jnp.float32)]
    meta = jnp.concatenate(lines, axis=0)
    for s in range(group):
        pay[s, pl.ds(base, extra), :] = meta
    y_copy.wait()


def last_kernel(parts, sol_in, arrived, rhs, diag, sol, b_buf, d_buf, y_buf, small, d_sem):
    rows = b_buf.shape[0]
    d_copies = chunked(diag.at[2], d_buf, d_sem, parts)
    b_copy = pltpu.make_async_copy(rhs.at[2], b_buf, small.at[0])
    b_copy.start()
    for copy in d_copies:
        copy.start()
    b_copy.wait()
    both = split_cols(b_buf[...] - (arrived[0] + arrived[1]))
    size = rows // parts
    outs = []
    for c in range(parts):
        at = pl.ds(c * size, size)
        d_copies[c].wait()
        y_buf[at, :] = dot3(d_buf[at, :], both)
        outs.append(pltpu.make_async_copy(y_buf.at[at], sol.at[2, at], small.at[1 + c]))
        outs[c].start()
    for copy in outs:
        copy.wait()


def sum_kernel(seg, got, out, meta):
    group = got.shape[0]
    base = 2 * seg
    extra = got.shape[1] - base
    for q in range(group):
        meta[q] = got[q, pl.ds(base, extra), :]

    def one(i, carry):
        wanted = i.astype(jnp.float32)
        total = jnp.zeros((seg, LANES), jnp.float32)
        for q in range(group):
            for k in range(2):
                line = got[q, pl.ds(base + k, 1), :]
                mask = jnp.broadcast_to(line, (seg, LANES)) == wanted
                total += jnp.where(mask, got[q, pl.ds(k * seg, seg), :], 0.0)
        out[i] = total
        return carry

    lax.fori_loop(0, out.shape[0], one, 0)


def weights_kernel(group, parts, rhs, tiles, dest, half, mine, other, share, u_vec,
                   b_buf, l0_buf, l1_buf, small, l0_sem, l1_sem):
    rows = b_buf.shape[0]
    count = rows // LANES
    copies = [
        chunked(tiles.at[1, 0], l0_buf, l0_sem, parts),
        chunked(tiles.at[1, 1], l1_buf, l1_sem, parts),
    ]
    b_copy = pltpu.make_async_copy(rhs.at[2], b_buf, small.at[0])
    b_copy.start()
    for per_tile in copies:
        for copy in per_tile:
            copy.start()
    b_copy.wait()
    own = mine[half[1]]
    share[...] = jnp.broadcast_to(
        left_product(own[2 : 2 + count, :], b_buf, rows), share.shape
    )
    total = None
    for k, buf in enumerate((l0_buf, l1_buf)):
        target = dest[1, 0, k]
        place = lax.rem(target, group)
        same = (target >= group) == (half[0] > 0)
        vector = jnp.where(same, mine[place], other[place])
        for copy in copies[k]:
            copy.wait()
        term = left_product(vector[2 : 2 + count, :], buf, rows)
        total = term if total is None else total + term
    lines = [total[:, r * LANES : (r + 1) * LANES] for r in range(count)]
    pad = u_vec.shape[0] - count
    if pad:
        lines.append(jnp.zeros((pad, LANES), jnp.float32))
    u_vec[...] = jnp.concatenate(lines, axis=0)


def cost(flops, size):
    return pl.CostEstimate(flops=flops, bytes_accessed=size, transcendentals=0)


def body(rhs, diag_inv, tiles, dest, obs_weight):
    count = lax.axis_size("rows")
    group = count // 2
    levels, rows, width = rhs.shape
    seg = rows // group
    lines = rows // LANES
    extra = -(-(lines + 2) // SUB) * SUB
    parts = 4
    f32 = jnp.float32
    place = lax.axis_index("rows")
    halves = [list(range(group)), list(range(group, count))]
    across = [(i, (i + group) % count) for i in range(count)]
    half = jnp.stack([place // group, place % group]).astype(jnp.int32)

    block = pltpu.VMEM((rows, width), f32)
    square = pltpu.VMEM((rows, rows), f32)
    sems = pltpu.SemaphoreType.DMA((parts,))
    params = pltpu.CompilerParams(vmem_limit_bytes=48 << 20)
    sol_shape = jax.ShapeDtypeStruct(rhs.shape, f32)
    mat_flops = 2 * rows * rows * width
    mat_bytes = 4 * rows * rows

    def exchange(pay):
        return lax.all_to_all(
            pay, "rows", split_axis=0, concat_axis=0, tiled=True, axis_index_groups=halves
        )

    def spread(partial_sums):
        back = lax.all_to_all(partial_sums, "rows", split_axis=0, concat_axis=0, tiled=True)
        return back.reshape(2, rows, width)

    def summed(got, extra):
        return pl.pallas_call(
            functools.partial(sum_kernel, seg),
            out_shape=(
                jax.ShapeDtypeStruct((count, seg, width), f32),
                jax.ShapeDtypeStruct((group, extra, width), f32),
            ),
            in_specs=[VMEM],
            out_specs=(VMEM, VMEM),
            cost_estimate=cost(2 * count * rows * width, 4 * 4 * rows * width),
            name="sum_parts",
        )(got)

    pad = -(-lines // SUB) * SUB - lines
    weight = jnp.pad(obs_weight.reshape(lines, LANES), ((0, pad), (0, 0)))
    sol, pay = pl.pallas_call(
        functools.partial(first_kernel, group, parts),
        out_shape=(sol_shape, jax.ShapeDtypeStruct((group, 2 * seg + extra, width), f32)),
        in_specs=[ANY, ANY, ANY, VMEM, SMEM],
        out_specs=(ANY, VMEM),
        scratch_shapes=[
            block, square, square, square, square, block,
            pltpu.SemaphoreType.DMA((2,)), sems, sems, sems, sems,
        ],
        compiler_params=params,
        cost_estimate=cost(3 * mat_flops, 4 * mat_bytes),
        name="level_first",
    )(rhs, diag_inv, tiles, weight, dest)

    got = exchange(pay)
    sums, mine = summed(got, extra)
    other = lax.ppermute(mine, "rows", across)
    arrived = spread(sums)

    share, u_vec = pl.pallas_call(
        functools.partial(weights_kernel, group, parts),
        out_shape=(
            jax.ShapeDtypeStruct((SUB, width), f32),
            jax.ShapeDtypeStruct((lines + pad, LANES), f32),
        ),
        in_specs=[ANY, ANY, SMEM, SMEM, VMEM, VMEM],
        out_specs=(VMEM, VMEM),
        scratch_shapes=[block, square, square, pltpu.SemaphoreType.DMA((1,)), sems, sems],
        compiler_params=params,
        cost_estimate=cost(4 * rows * rows, 2 * mat_bytes),
        name="weights",
    )(rhs, tiles, dest, half, mine, other)

    sol, pay = pl.pallas_call(
        functools.partial(middle_kernel, group, parts),
        out_shape=(sol_shape, jax.ShapeDtypeStruct((group, 2 * seg + SUB, width), f32)),
        in_specs=[ANY, VMEM, ANY, ANY, ANY, VMEM, VMEM, SMEM],
        out_specs=(ANY, VMEM),
        scratch_shapes=[
            block, square, square, square, block,
            pltpu.SemaphoreType.DMA((2,)), sems, sems, sems,
        ],
        input_output_aliases={0: 0},
        compiler_params=params,
        cost_estimate=cost(3 * mat_flops, 3 * mat_bytes),
        name="level_middle",
    )(sol, arrived, rhs, diag_inv, tiles, share, u_vec, dest)

    got = exchange(pay)
    sums, mine = summed(got, SUB)
    near = jnp.sum(mine[:, 2, :], axis=0)
    far = lax.ppermute(near, "rows", across)
    observed = near + far
    arrived = spread(sums)

    sol = pl.pallas_call(
        functools.partial(last_kernel, parts),
        out_shape=sol_shape,
        in_specs=[ANY, VMEM, ANY, ANY],
        out_specs=ANY,
        scratch_shapes=[block, square, block, pltpu.SemaphoreType.DMA((1 + parts,)), sems],
        input_output_aliases={0: 0},
        compiler_params=params,
        cost_estimate=cost(mat_flops, mat_bytes),
        name="level_last",
    )(sol, arrived, rhs, diag_inv)
    return sol, observed


def solution(mesh):
    in_specs = (
        P(None, "rows", "parts"),
        P(None, "rows", None),
        P(None, "rows", None, None),
        P(None, "rows", None),
        P("rows"),
    )
    out_specs = (P(None, "rows", "parts"), P("parts"))
    return jax.shard_map(body, mesh=mesh, in_specs=in_specs, out_specs=out_specs, check_vma=False)
```

time: 157 us -> 117 us (0.75)
  blocking collectives: 77.9 us -> 34.1 us
  Pallas kernels: 0 us -> 27 us
  matrix products: 24.5 us -> 0 us
  waiting for transfers between devices: 30.5 us -> 36.6 us
  starting transfers between devices: 16.5 us -> 13.5 us
  local copies, waits for them, and re-layouts: 5.05 us -> 2.65 us
    ppermute x0 -> x2, waiting for transfers between devices: none -> 36.6 us  [the longest x1 19.3 us: body(): other = lax.ppermute(mine, 'rows', across)]
    psum x1 -> x0, blocking collectives: 32 us -> none  [body(): observed = lax.psum(partial_sum, 'rows')]
    all_to_all x3 -> x2, waiting for transfers between devices: 30.5 us -> 0.01 us  [spread(): lax.all_to_all(partial_sums, 'rows', split_axis=0, concat_axis=0, tiled=T...]
    all_gather x1 -> x0, blocking collectives: 29.2 us -> none  [body(): pattern = lax.all_gather(dest, 'rows', axis=1, tiled=True)]
    pallas_call x0 -> x6, Pallas kernels: none -> 27 us  [the longest x1 7.39 us: body(): pl.pallas_call(functools.partial(first_kernel, group, parts), out_shape=(...]
    dot_general x8 -> x0, matrix products: 24.5 us -> none  [the longest x2 12.3 us: collect_updates(): jnp.einsum('kab,bc->kac', tiles_level, solved_block, precision=lax.Precis...]
    all_to_all x1 -> x2, blocking collectives: 16.7 us -> 34.1 us  [exchange(): lax.all_to_all(pay, 'rows', split_axis=0, concat_axis=0, tiled=True, axis...]
    all_to_all x3 -> x2, starting transfers between devices: 16.5 us -> 7.83 us  [spread(): lax.all_to_all(partial_sums, 'rows', split_axis=0, concat_axis=0, tiled=T...]
  transfers between devices with their start and end apart: 3 -> 4, of which waited for: 2 -> 2; matrix products, arithmetic and copies ran while one was open for 0% -> 1% of each run, Pallas kernels for 0% -> 3%
where the time goes in v1:
time: 117 us; the launch traced here: 116 us
  waiting for transfers between devices  36.6 us (31%)
  blocking collectives  34.1 us (29%)
  Pallas kernels  27 us (23%)
  starting transfers between devices  13.5 us (12%)
  local copies, waits for them, and re-layouts  2.65 us (2%)
  other arithmetic  1.37 us (1%)
    all_to_all x2, blocking collectives, exchange(): lax.all_to_all(pay, 'rows', split_axis=0, concat_axis=0, tiled=True, axis...  34.1 us
    ppermute x1, waiting for transfers between devices, body(): other = lax.ppermute(mine, 'rows', across)  19.3 us
    ppermute x1, waiting for transfers between devices, body(): far = lax.ppermute(near, 'rows', across)  17.3 us
    all_to_all x2, starting transfers between devices, spread(): lax.all_to_all(partial_sums, 'rows', split_axis=0, concat_axis=0, tiled=T...  7.83 us
    pallas_call x1, Pallas kernels, body(): pl.pallas_call(functools.partial(first_kernel, group, parts), out_shape=(...  7.39 us
    pallas_call x1, Pallas kernels, body(): pl.pallas_call(functools.partial(middle_kernel, group, parts), out_shape=...  6.53 us
    pallas_call x2, Pallas kernels, summed(): pl.pallas_call(functools.partial(sum_kernel, seg), out_shape=(jax.ShapeDt...  6.23 us
    pallas_call x1, Pallas kernels, body(): pl.pallas_call(functools.partial(weights_kernel, group, parts), out_shape...  3.63 us
  transfers between devices with their start and end apart: 4, of which 2 were waited for; matrix products, arithmetic and copies ran while one was open for 1% of the time, Pallas kernels for 3%

profile of v1, /device:TPU:0, one launch (start us, length us, event | category | flops | bytes accessed | tf_op | source)
XLA Modules:
  0.0 116.0 jit_solution(7127089684909218517)
XLA Ops:
  0.6 0.7 pad.4.weight
  1.3 0.0 copy-start
  1.3 1.3 %copy-done = f32[3,768,128]{2,1,0:T(8,128)S(1)} copy-done((f32[3,768,128]{2,1,0:T(8,128)S(1)}, f32[3,768,128]{2,1,0:T(8,128)}, u32[]{:S(2)}) %copy-start) | copy-done | bytes 1179672
  2.6 0.0 copy-start.3
  2.6 0.7 copy-done.3
  3.3 7.4 %level_first.1 = (f32[3,768,128]{2,1,0:T(8,128)}, f32[8,200,128]{2,1,0:T(8,128)S(1)}) custom-call(f32[3,768,128]{2,1,0:T(8,128)S(1)} %copy-done, f32[3,768,768]{2,1,0:T(8,128)} %diag.5, f32[2,2,768,768]{3,2,1,0:T(8,128)} %tiles.5, f32[8,128]{1,0:T(8,128)S(1)} %pad.4.weight, s32[2,1,2]{2,1,0:T(1,128)S(1)} %copy-done.3), custom_call_target="tpu_custom_call" | custom-call | flops 452984832 | bytes 9437184 | tf_op jit(solution)/shard_map/level_first/pallas_call | solution.py:273
  10.7 18.1 %all_to_all.20.got = f32[8,200,128]{2,1,0:T(8,128)} all-to-all(f32[8,200,128]{2,1,0:T(8,128)S(1)} %get-tuple-element.13), channel_id=1, replica_groups={{0,1,2,3,4,5,6,7},{8,9,10,11,12,13,14,15},{16,17,18,19,20,21,22,23},{24..., dimensions={0} | all-to-all | bytes 1638400 | tf_op jit(solution)/shard_map/all_to_all | solution.py:250
  28.7 0.0 copy-start.1
  28.7 0.0 copy-start.4
  28.7 3.2 %sum_parts.2 = (f32[16,96,128]{2,1,0:T(8,128)}, f32[8,8,128]{2,1,0:T(8,128)}) custom-call(f32[8,200,128]{2,1,0:T(8,128)} %all_to_all.20.got), custom_call_target="tpu_custom_call" | custom-call | flops 3145728 | bytes 1572864 | tf_op jit(solution)/shard_map/sum_parts/pallas_call | solution.py:259
  31.9 0.0 copy-start.2
  31.9 4.2 %all-to-all-start.1 = ((f32[16,96,128]{2,1,0:T(8,128)}), f32[16,96,128]{2,1,0:T(8,128)S(1)}, u32[]{:S(2)}, u32[]{:S(2)}) async-start(f32[16,96,128]{2,1,0:T(8,128)} %get-tuple-element.14), calls=%async_computation.1 | async-start | bytes 1572864 | tf_op jit(solution)/shard_map/all_to_all | solution.py:255
  36.2 0.0 copy-done.2
  36.2 2.9 %collective-permute-start = (f32[8,8,128]{2,1,0:T(8,128)S(1)}, f32[8,8,128]{2,1,0:T(8,128)S(1)}, u32[]{:S(2)}, u32[]{:S(2)}) collective-permute-start(f32[8,8,128]{2,1,0:T(8,128)S(1)} %copy-done.2), channel_id=1, source_target_pairs={{0,8},{1,9},{2,10},{3,11},{4,12},{5,13},{6,14},{7,15},{8,0},{9,1},... | collective-permute-start | bytes 98312 | tf_op jit(solution)/shard_map/ppermute | solution.py:289
  39.0 0.1 pad_add_fusion.half
  39.1 19.3 %collective-permute-done.other = f32[8,8,128]{2,1,0:T(8,128)S(1)} collective-permute-done((f32[8,8,128]{2,1,0:T(8,128)S(1)}, f32[8,8,128]{2,1,0:T(8,128)S(1)}, u32[]{:S(2)}, u32[]{:S(2)}) %collective-permute-start) | collective-permute-done | bytes 32800 | tf_op jit(solution)/shard_map/ppermute | solution.py:289
  58.4 0.0 copy-done.1
  58.4 0.0 copy-done.4
  58.4 3.6 %weights.1 = (f32[8,128]{1,0:T(8,128)S(1)}, f32[8,128]{1,0:T(8,128)S(1)}) custom-call(f32[3,768,128]{2,1,0:T(8,128)S(1)} %copy-done.1, f32[2,2,768,768]{3,2,1,0:T(8,128)} %tiles.5, s32[2,1,2]{2,1,0:T(1,128)S(1)} %copy-done.4, s32[2]{0:T(128)S(1)} %pad_add_fusion.half, f32[8,8,128]{2,1,0:T(8,128)S(1)} %copy-done.2, f32[8,8,128]{2,1,0:T(8,128)S(1)} %collective-permute-done.other), custom_call_target="tpu_custom_call" | custom-call | flops 2359296 | bytes 4718592 | tf_op jit(solution)/shard_map/weights/pallas_call | solution.py:292
  62.1 0.0 all-to-all-done.1
  62.1 6.5 %level_middle.1 = (f32[3,768,128]{2,1,0:T(8,128)}, f32[8,200,128]{2,1,0:T(8,128)S(1)}) custom-call(f32[3,768,128]{2,1,0:T(8,128)} %get-tuple-element.12.sol_in, f32[2,768,128]{2,1,0:T(8,128)S(1)} %bitcast.5, f32[3,768,128]{2,1,0:T(8,128)S(1)} %copy-done.1, f32[3,768,768]{2,1,0:T(8,128)} %diag.5, ...), custom_call_target="tpu_custom_call", output_to_operand_aliasing={{0}: (0, {})} | custom-call | flops 452984832 | bytes 7077888 | tf_op jit(solution)/shard_map/level_middle/pallas_call | solution.py:306
  68.6 16.0 %all_to_all.21.got = f32[8,200,128]{2,1,0:T(8,128)} all-to-all(f32[8,200,128]{2,1,0:T(8,128)S(1)} %get-tuple-element.19), channel_id=1, replica_groups={{0,1,2,3,4,5,6,7},{8,9,10,11,12,13,14,15},{16,17,18,19,20,21,22,23},{24..., dimensions={0} | all-to-all | bytes 1638400 | tf_op jit(solution)/shard_map/all_to_all | solution.py:250
  84.6 3.1 %sum_parts.3 = (f32[16,96,128]{2,1,0:T(8,128)}, f32[8,8,128]{2,1,0:T(8,128)}) custom-call(f32[8,200,128]{2,1,0:T(8,128)} %all_to_all.21.got), custom_call_target="tpu_custom_call" | custom-call | flops 3145728 | bytes 1572864 | tf_op jit(solution)/shard_map/sum_parts/pallas_call | solution.py:259
  87.7 3.6 %all-to-all-start.3 = ((f32[16,96,128]{2,1,0:T(8,128)}), f32[16,96,128]{2,1,0:T(8,128)S(1)}, u32[]{:S(2)}, u32[]{:S(2)}) async-start(f32[16,96,128]{2,1,0:T(8,128)} %get-tuple-element.20), calls=%async_computation.3 | async-start | bytes 1572864 | tf_op jit(solution)/shard_map/all_to_all | solution.py:255
  91.3 0.8 slice_reduce_fusion
  92.1 2.8 %collective-permute-start.1 = (f32[128]{0:T(128)S(1)}, f32[128]{0:T(128)S(1)}, u32[]{:S(2)}, u32[]{:S(2)}) collective-permute-start(f32[128]{0:T(128)S(1)} %slice_reduce_fusion), channel_id=1, source_target_pairs={{0,8},{1,9},{2,10},{3,11},{4,12},{5,13},{6,14},{7,15},{8,0},{9,1},... | collective-permute-start | bytes 1544 | tf_op jit(solution)/shard_map/ppermute | solution.py:324
  94.9 17.3 %collective-permute-done.1 = f32[128]{0:T(128)S(1)} collective-permute-done((f32[128]{0:T(128)S(1)}, f32[128]{0:T(128)S(1)}, u32[]{:S(2)}, u32[]{:S(2)}) %collective-permute-start.1) | collective-permute-done | bytes 544 | tf_op jit(solution)/shard_map/ppermute | solution.py:324
  112.2 0.5 add.11
  112.7 0.0 all-to-all-done.3
  112.7 3.3 %level_last.1 = f32[3,768,128]{2,1,0:T(8,128)} custom-call(f32[3,768,128]{2,1,0:T(8,128)} %get-tuple-element.18.sol_in, f32[2,768,128]{2,1,0:T(8,128)S(1)} %bitcast.6, f32[3,768,128]{2,1,0:T(8,128)S(1)} %copy-done.1, f32[3,768,768]{2,1,0:T(8,128)} %diag.5), custom_call_target="tpu_custom_call", output_to_operand_aliasing={{}: (0, {})} | custom-call | flops 150994944 | bytes 2359296 | tf_op jit(solution)/shard_map/level_last/pallas_call | solution.py:328
Async XLA Ops:
  1.3 1.3 %copy-start = (f32[3,768,128]{2,1,0:T(8,128)S(1)}, f32[3,768,128]{2,1,0:T(8,128)}, u32[]{:S(2)}) copy-start(f32[3,768,128]{2,1,0:T(8,128)} %rhs.7) | copy-start | bytes 3538948
  2.6 0.7 copy-start.3
  28.7 29.7 %copy-start.1 = (f32[3,768,128]{2,1,0:T(8,128)S(1)}, f32[3,768,128]{2,1,0:T(8,128)}, u32[]{:S(2)}) copy-start(f32[3,768,128]{2,1,0:T(8,128)} %rhs.7) | copy-start | bytes 3538948
  28.7 29.7 %copy-start.4 = (s32[2,1,2]{2,1,0:T(1,128)S(1)}, s32[2,1,2]{2,1,0:T(1,128)}, u32[]{:S(2)}) copy-start(s32[2,1,2]{2,1,0:T(1,128)} %dest.5) | copy-start | bytes 52
  31.9 4.2 %copy-start.2 = (f32[8,8,128]{2,1,0:T(8,128)S(1)}, f32[8,8,128]{2,1,0:T(8,128)}, u32[]{:S(2)}) copy-start(f32[8,8,128]{2,1,0:T(8,128)} %get-tuple-element.15.mine) | copy-start | bytes 98308
  31.9 30.2 %all-to-all-start.1 = ((f32[16,96,128]{2,1,0:T(8,128)}), f32[16,96,128]{2,1,0:T(8,128)S(1)}, u32[]{:S(2)}, u32[]{:S(2)}) async-start(f32[16,96,128]{2,1,0:T(8,128)} %get-tuple-element.14), calls=%async_computation.1 | async-start | bytes 1572864 | tf_op jit(solution)/shard_map/all_to_all | solution.py:255
  36.2 22.3 %collective-permute-start = (f32[8,8,128]{2,1,0:T(8,128)S(1)}, f32[8,8,128]{2,1,0:T(8,128)S(1)}, u32[]{:S(2)}, u32[]{:S(2)}) collective-permute-start(f32[8,8,128]{2,1,0:T(8,128)S(1)} %copy-done.2), channel_id=1, source_target_pairs={{0,8},{1,9},{2,10},{3,11},{4,12},{5,13},{6,14},{7,15},{8,0},{9,1},... | collective-permute-start | bytes 98312 | tf_op jit(solution)/shard_map/ppermute | solution.py:289
  87.7 25.0 %all-to-all-start.3 = ((f32[16,96,128]{2,1,0:T(8,128)}), f32[16,96,128]{2,1,0:T(8,128)S(1)}, u32[]{:S(2)}, u32[]{:S(2)}) async-start(f32[16,96,128]{2,1,0:T(8,128)} %get-tuple-element.20), calls=%async_computation.3 | async-start | bytes 1572864 | tf_op jit(solution)/shard_map/all_to_all | solution.py:255
  92.1 20.1 %collective-permute-start.1 = (f32[128]{0:T(128)S(1)}, f32[128]{0:T(128)S(1)}, u32[]{:S(2)}, u32[]{:S(2)}) collective-permute-start(f32[128]{0:T(128)S(1)} %slice_reduce_fusion), channel_id=1, source_target_pairs={{0,8},{1,9},{2,10},{3,11},{4,12},{5,13},{6,14},{7,15},{8,0},{9,1},... | collective-permute-start | bytes 1544 | tf_op jit(solution)/shard_map/ppermute | solution.py:324

commit v2 on v1

v2 whole, which is shorter than its diff:
```python
import functools

import jax
import jax.numpy as jnp
from jax import lax
from jax.experimental import pallas as pl
from jax.experimental.pallas import tpu as pltpu
from jax.sharding import PartitionSpec as P

LANES = 128
SUB = 8
HBM = pl.BlockSpec(memory_space=pltpu.HBM)
ANY = pl.BlockSpec(memory_space=pl.ANY)
VMEM = pl.BlockSpec(memory_space=pltpu.VMEM)
SMEM = pl.BlockSpec(memory_space=pltpu.SMEM)


def split(x):
    hi = x.astype(jnp.bfloat16)
    lo = (x - hi.astype(jnp.float32)).astype(jnp.bfloat16)
    return hi, lo


def split_cols(x):
    hi, lo = split(x)
    return jnp.concatenate([hi, lo], axis=1)


def dot_terms(hi, lo, both):
    width = both.shape[1] // 2
    wide = jnp.dot(hi, both, preferred_element_type=jnp.float32)
    narrow = jnp.dot(lo, both[:, :width], preferred_element_type=jnp.float32)
    return wide[:, :width] + (wide[:, width:] + narrow)


def dot_late(hi, lo_ref, lo_copy, both):
    width = both.shape[1] // 2
    wide = jnp.dot(hi, both, preferred_element_type=jnp.float32)
    lo_copy.wait()
    narrow = jnp.dot(lo_ref[...], both[:, :width], preferred_element_type=jnp.float32)
    return wide[:, :width] + (wide[:, width:] + narrow)


def left_product(vector, matrix, rows):
    columns = vector.T
    total = None
    for r in range(rows // LANES):
        block = matrix[r * LANES : (r + 1) * LANES, :]
        term = jnp.sum(columns[:, r : r + 1] * block, axis=0, keepdims=True)
        total = term if total is None else total + term
    return total


def chunked(ref, buf, sem, parts):
    size = buf.shape[0] // parts
    copies = []
    for c in range(parts):
        at = pl.ds(c * size, size)
        copies.append(pltpu.make_async_copy(ref.at[at], buf.at[at], sem.at[c]))
    return copies


def put_slots(pay, k, seg, first, out):
    for s in range(out.shape[0] // seg):
        pay[first + s, pl.ds(k * seg, seg), :] = out[s * seg : (s + 1) * seg]


def first_kernel(
    group, parts, rhs, diag, tiles, weight, dest, sol, pay,
    b_buf, d_buf, l0_buf, l1_buf, v_buf, y_buf, w_buf, i_buf, small, d_sem, l0_sem, l1_sem, v_sem,
):
    rows = b_buf.shape[0]
    seg = rows // group
    size = rows // parts
    d_copies = chunked(diag.at[0], d_buf, d_sem, parts)
    l_copies = [
        chunked(tiles.at[0, 0], l0_buf, l0_sem, parts),
        chunked(tiles.at[0, 1], l1_buf, l1_sem, parts),
    ]
    v_copies = chunked(diag.at[2], v_buf, v_sem, parts)
    b_copy = pltpu.make_async_copy(rhs.at[0], b_buf, small.at[0])
    w_copy = pltpu.make_async_copy(weight, w_buf, small.at[2])
    i_copy = pltpu.make_async_copy(dest, i_buf, small.at[3])
    b_copy.start()
    for copies in (d_copies, *l_copies, v_copies):
        for copy in copies:
            copy.start()
    w_copy.start()
    i_copy.start()
    b_copy.wait()
    both = split_cols(b_buf[...])
    for c in range(parts):
        at = pl.ds(c * size, size)
        d_copies[c].wait()
        y_buf[at, :] = dot_terms(*split(d_buf[at, :]), both)
    y_copy = pltpu.make_async_copy(y_buf, sol.at[0], small.at[1])
    y_copy.start()
    both = split_cols(y_buf[...])
    for k, buf in enumerate((l0_buf, l1_buf)):
        for c in range(parts):
            l_copies[k][c].wait()
            out = dot_terms(*split(buf[pl.ds(c * size, size), :]), both)
            put_slots(pay, k, seg, c * (size // seg), out)
    w_copy.wait()
    i_copy.wait()
    for copy in v_copies:
        copy.wait()
    vector = left_product(w_buf[...], v_buf, rows)
    base = 2 * seg
    extra = pay.shape[1] - base
    lines = [jnp.full((1, LANES), i_buf[0, 0, k].astype(jnp.float32)) for k in range(2)]
    lines += [vector[:, r * LANES : (r + 1) * LANES] for r in range(rows // LANES)]
    if extra > len(lines):
        lines.append(jnp.zeros((extra - len(lines), LANES), jnp.float32))
    meta = jnp.concatenate(lines, axis=0)
    for s in range(group):
        pay[s, pl.ds(base, extra), :] = meta
    y_copy.wait()


def fold_kernel(group, rhs, diag, tiles, mine, half, m0_hi, m1_hi, m_lo, bias, share,
                d_buf, l_buf, t_buf, o_hi, o_lo, d_sem, l_sem, small, o_sem):
    rows = d_buf.shape[0]
    parts = d_sem.shape[0]
    size = rows // parts
    d_copies = chunked(diag.at[1], d_buf, d_sem, parts)
    l_copies = [chunked(tiles.at[1, k], l_buf.at[k], l_sem.at[k], parts) for k in range(2)]
    copies = [
        pltpu.make_async_copy(rhs.at[1], bias, small.at[0]),
        pltpu.make_async_copy(rhs.at[2], t_buf, small.at[1]),
    ]
    for copy in (*d_copies, *l_copies[0], *l_copies[1], *copies):
        copy.start()
    for copy in d_copies:
        copy.wait()
    d_hi, d_lo = split(d_buf[...])
    d_both = jnp.concatenate([d_hi, d_lo], axis=1)
    puts = []
    for k in range(2):
        for c in range(parts):
            at = pl.ds(c * size, size)
            l_copies[k][c].wait()
            out = dot_terms(*split(l_buf[k, at, :]), d_both)
            hi, lo = split(out)
            o_lo[k, at, :] = lo
            puts.append(
                pltpu.make_async_copy(o_lo.at[k, at], m_lo.at[k, at], o_sem.at[k, c])
            )
            puts[-1].start()
            if k == 0:
                m0_hi[at, :] = hi
            else:
                o_hi[at, :] = hi
                puts.append(pltpu.make_async_copy(o_hi.at[at], m1_hi.at[at], o_sem.at[2, c]))
                puts[-1].start()
    for copy in copies:
        copy.wait()
    share[...] = left_product(mine[half[1]][2 : 2 + rows // LANES, :], t_buf, rows)
    for copy in puts:
        copy.wait()


def middle_kernel(
    group, arrived, bias, m0_hi, m1_hi, m_lo, share, mine, other, dest, half,
    pay, rest, o_hi, o_lo, sem,
):
    rows = bias.shape[0]
    seg = rows // group
    count = rows // LANES
    lo_copies = [pltpu.make_async_copy(m_lo.at[k], o_lo.at[k], sem.at[k]) for k in range(2)]
    hi_copy = pltpu.make_async_copy(m1_hi, o_hi, sem.at[2])
    for copy in (lo_copies[0], hi_copy, lo_copies[1]):
        copy.start()
    rest[...] = bias[...] - (arrived[0] + arrived[1])
    both = split_cols(rest[...])
    part = share[...]
    for k, hi in enumerate((m0_hi, o_hi)):
        if k == 1:
            hi_copy.wait()
        out = dot_late(hi[...], o_lo.at[k], lo_copies[k], both)
        put_slots(pay, k, seg, 0, out)
        target = dest[1, 0, k]
        place = lax.rem(target, group)
        same = (target >= group) == (half[0] > 0)
        vector = jnp.where(same, mine[place], other[place])
        part = part - left_product(vector[2 : 2 + count, :], out, rows)
    base = 2 * seg
    extra = pay.shape[1] - base
    lines = [jnp.full((1, LANES), dest[1, 0, k].astype(jnp.float32)) for k in range(2)]
    lines += [part, jnp.zeros((extra - 3, LANES), jnp.float32)]
    meta = jnp.concatenate(lines, axis=0)
    for s in range(group):
        pay[s, pl.ds(base, extra), :] = meta


def window_kernel(parts, sol_in, rest, rhs, diag, sol, d_hi, d_lo, bias,
                  d_buf, y_buf, lo_buf, d_sem, small):
    rows = y_buf.shape[0]
    copies = [chunked(diag.at[1 + j], d_buf.at[j], d_sem.at[j], parts) for j in range(2)]
    b_copy = pltpu.make_async_copy(rhs.at[2], bias, small.at[0])
    for copy in (*copies[0], *copies[1], b_copy):
        copy.start()
    both = split_cols(rest[...])
    size = rows // parts
    for c in range(parts):
        at = pl.ds(c * size, size)
        copies[0][c].wait()
        y_buf[at, :] = dot_terms(*split(d_buf[0, at, :]), both)
    y_copy = pltpu.make_async_copy(y_buf, sol.at[1], small.at[1])
    y_copy.start()
    for c in range(parts):
        at = pl.ds(c * size, size)
        copies[1][c].wait()
        hi, lo = split(d_buf[1, at, :])
        d_hi[at, :] = hi
        lo_buf[at, :] = lo
    lo_copy = pltpu.make_async_copy(lo_buf, d_lo, small.at[2])
    lo_copy.start()
    lo_copy.wait()
    b_copy.wait()
    y_copy.wait()


def last_kernel(parts, sol_in, arrived, bias, d_hi, d_lo, near, far, sol, seen,
                y_buf, lo_buf, sem, lo_sem):
    rows = y_buf.shape[0]
    lo_copies = chunked(d_lo, lo_buf, lo_sem, parts)
    for copy in lo_copies:
        copy.start()
    both = split_cols(bias[...] - (arrived[0] + arrived[1]))
    size = rows // parts
    outs = []
    for c in range(parts):
        at = pl.ds(c * size, size)
        y_buf[at, :] = dot_late(d_hi[at, :], lo_buf.at[at], lo_copies[c], both)
        outs.append(pltpu.make_async_copy(y_buf.at[at], sol.at[2, at], sem.at[c]))
        outs[c].start()
    seen[...] = near[...] + far[...]
    for copy in outs:
        copy.wait()


def sum_kernel(seg, got, out, tail, where, sem):
    group = got.shape[0]
    base = 2 * seg
    copies = [
        pltpu.make_async_copy(got.at[q, pl.ds(base, 2)], where.at[q], sem.at[q])
        for q in range(group)
    ]
    for copy in copies:
        copy.start()
    out[...] = jnp.zeros_like(out)
    if tail.shape[0] == 1:
        total = got[0, base + 2 : base + 3, :]
        for q in range(1, group):
            total = total + got[q, base + 2 : base + 3, :]
        tail[...] = total
    else:
        for q in range(group):
            tail[q] = got[q, base:, :]
    for q in range(group):
        copies[q].wait()
        for k in range(2):
            target = where[q, k, 0].astype(jnp.int32)
            out[target] += got[q, pl.ds(k * seg, seg), :]


def cost(flops, size):
    return pl.CostEstimate(flops=flops, bytes_accessed=size, transcendentals=0)


def limit(mib):
    return pltpu.CompilerParams(vmem_limit_bytes=mib << 20)


def body(rhs, diag_inv, tiles, dest, obs_weight):
    count = lax.axis_size("rows")
    group = count // 2
    levels, rows, width = rhs.shape
    seg = rows // group
    lines = rows // LANES
    extra = -(-(lines + 2) // SUB) * SUB
    parts = 2
    f32 = jnp.float32
    place = lax.axis_index("rows")
    halves = [list(range(group)), list(range(group, count))]
    across = [(i, (i + group) % count) for i in range(count)]
    half = jnp.stack([place // group, place % group]).astype(jnp.int32)

    def stay(x):
        return pltpu.with_memory_space_constraint(x, pltpu.HBM)

    block = pltpu.VMEM((rows, width), f32)
    square = pltpu.VMEM((rows, rows), f32)
    sems = pltpu.SemaphoreType.DMA((parts,))
    sol_shape = jax.ShapeDtypeStruct(rhs.shape, f32)
    term = jax.ShapeDtypeStruct((rows, rows), jnp.bfloat16)
    flat = jax.ShapeDtypeStruct((rows, width), f32)
    line = jax.ShapeDtypeStruct((1, width), f32)
    mat_flops = 2 * rows * rows * width
    mat_bytes = 4 * rows * rows

    def exchange(pay):
        return lax.all_to_all(
            pay, "rows", split_axis=0, concat_axis=0, tiled=True, axis_index_groups=halves
        )

    def spread(partial_sums):
        back = lax.all_to_all(partial_sums, "rows", split_axis=0, concat_axis=0, tiled=True)
        return back.reshape(2, rows, width)

    def summed(got, tail):
        return pl.pallas_call(
            functools.partial(sum_kernel, seg),
            out_shape=(
                jax.ShapeDtypeStruct((count, seg, width), f32),
                jax.ShapeDtypeStruct(tail, f32),
            ),
            in_specs=[VMEM],
            out_specs=(VMEM, VMEM),
            scratch_shapes=[
                pltpu.SMEM((group, 2, width), f32),
                pltpu.SemaphoreType.DMA((group,)),
            ],
            compiler_params=limit(6),
            cost_estimate=cost(2 * rows * width, 4 * 4 * rows * width),
            name="sum_parts",
        )(got)

    sol, pay = pl.pallas_call(
        functools.partial(first_kernel, group, parts),
        out_shape=(sol_shape, jax.ShapeDtypeStruct((group, 2 * seg + extra, width), f32)),
        in_specs=[HBM, HBM, HBM, HBM, HBM],
        out_specs=(HBM, VMEM),
        scratch_shapes=[
            block, square, square, square, square, block,
            pltpu.VMEM((lines, LANES), f32), pltpu.SMEM(dest.shape, jnp.int32),
            pltpu.SemaphoreType.DMA((4,)), sems, sems, sems, sems,
        ],
        compiler_params=limit(24),
        cost_estimate=cost(3 * mat_flops, 4 * mat_bytes),
        name="level_first",
    )(stay(rhs), stay(diag_inv), stay(tiles), stay(obs_weight.reshape(lines, LANES)), stay(dest))

    got = exchange(pay)
    sums, mine = summed(got, (group, extra, width))
    sums, diag_later, tiles_later, rhs_later = lax.optimization_barrier(
        (sums, diag_inv, tiles, rhs)
    )
    other = lax.ppermute(mine, "rows", across)
    arrived = spread(sums)
    m0_hi, m1_hi, m_lo, bias, share = pl.pallas_call(
        functools.partial(fold_kernel, group),
        out_shape=(term, term, jax.ShapeDtypeStruct((2, rows, rows), jnp.bfloat16), flat, line),
        in_specs=[HBM, HBM, HBM, VMEM, SMEM],
        out_specs=(VMEM, HBM, HBM, VMEM, VMEM),
        scratch_shapes=[
            square, pltpu.VMEM((2, rows, rows), f32), block,
            pltpu.VMEM((rows, rows), jnp.bfloat16), pltpu.VMEM((2, rows, rows), jnp.bfloat16),
            sems, pltpu.SemaphoreType.DMA((2, parts)), pltpu.SemaphoreType.DMA((2,)),
            pltpu.SemaphoreType.DMA((3, parts)),
        ],
        compiler_params=limit(40),
        cost_estimate=cost(6 * rows * mat_flops // width, 3 * mat_bytes),
        name="fold_levels",
    )(stay(rhs_later), stay(diag_later), stay(tiles_later), mine, half)

    pay, rest = pl.pallas_call(
        functools.partial(middle_kernel, group),
        out_shape=(jax.ShapeDtypeStruct((group, 2 * seg + SUB, width), f32), flat),
        in_specs=[VMEM, VMEM, VMEM, HBM, HBM, VMEM, VMEM, VMEM, SMEM, SMEM],
        out_specs=(VMEM, VMEM),
        scratch_shapes=[
            pltpu.VMEM((rows, rows), jnp.bfloat16), pltpu.VMEM((2, rows, rows), jnp.bfloat16),
            pltpu.SemaphoreType.DMA((3,)),
        ],
        compiler_params=limit(16),
        cost_estimate=cost(2 * mat_flops, 2 * mat_bytes),
        name="level_middle",
    )(arrived, bias, m0_hi, stay(m1_hi), stay(m_lo), share, mine, other, dest, half)

    pay, diag_later, rhs_later = lax.optimization_barrier((pay, diag_inv, rhs))
    got = exchange(pay)
    sums, near = summed(got, (1, width))
    far = lax.ppermute(near, "rows", across)
    arrived = spread(sums)
    sol, d_hi, d_lo, bias = pl.pallas_call(
        functools.partial(window_kernel, parts),
        out_shape=(sol_shape, term, term, flat),
        in_specs=[HBM, VMEM, HBM, HBM],
        out_specs=(HBM, VMEM, HBM, VMEM),
        scratch_shapes=[
            pltpu.VMEM((2, rows, rows), f32), block, pltpu.VMEM((rows, rows), jnp.bfloat16),
            pltpu.SemaphoreType.DMA((2, parts)), pltpu.SemaphoreType.DMA((3,)),
        ],
        input_output_aliases={0: 0},
        compiler_params=limit(32),
        cost_estimate=cost(mat_flops, 2 * mat_bytes),
        name="in_window",
    )(sol, rest, stay(rhs_later), stay(diag_later))

    sol, seen = pl.pallas_call(
        functools.partial(last_kernel, parts),
        out_shape=(sol_shape, jax.ShapeDtypeStruct((1, width), f32)),
        in_specs=[HBM, VMEM, VMEM, VMEM, HBM, VMEM, VMEM],
        out_specs=(HBM, VMEM),
        scratch_shapes=[
            block, pltpu.VMEM((rows, rows), jnp.bfloat16), pltpu.SemaphoreType.DMA((parts,)), sems,
        ],
        input_output_aliases={0: 0},
        compiler_params=limit(16),
        cost_estimate=cost(mat_flops, mat_bytes),
        name="level_last",
    )(sol, arrived, bias, d_hi, stay(d_lo), near, far)
    return sol, seen.reshape(width)


def solution(mesh):
    in_specs = (
        P(None, "rows", "parts"),
        P(None, "rows", None),
        P(None, "rows", None, None),
        P(None, "rows", None),
        P("rows"),
    )
    out_specs = (P(None, "rows", "parts"), P("parts"))
    return jax.shard_map(body, mesh=mesh, in_specs=in_specs, out_specs=out_specs, check_vma=False)
```

time: 117 us -> 104 us (0.89)
  waiting for transfers between devices: 36.6 us -> 14.2 us
  Pallas kernels: 27 us -> 37.1 us
  other arithmetic: 1.37 us -> 0.08 us
    ppermute x1, waiting for transfers between devices: 19.3 us -> 0.14 us  [body(): other = lax.ppermute(mine, 'rows', across)]
    pallas_call x3 -> x4, Pallas kernels: 13.4 us -> 27.9 us  [the longest x1 16.8 us: body(): pl.pallas_call(functools.partial(fold_kernel, group), out_shape=(term, te...]
    ppermute x1, waiting for transfers between devices: 17.3 us -> 14 us  [body(): far = lax.ppermute(near, 'rows', across)]
    pallas_call x2, Pallas kernels: 6.23 us -> 3.42 us  [summed(): pl.pallas_call(functools.partial(sum_kernel, seg), out_shape=(jax.ShapeDt...]
    pallas_call x1, Pallas kernels: 7.39 us -> 5.71 us  [body(): pl.pallas_call(functools.partial(first_kernel, group, parts), out_shape=(...]
    unnamed x10 -> x8, local copies, waits for them, and re-layouts: 1.96 us -> 3.48 us
  transfers between devices with their start and end apart: 4 -> 4, of which waited for: 2 -> 2; matrix products, arithmetic and copies ran while one was open for 1% -> 0% of each run, Pallas kernels for 3% -> 19%
where the time goes in v2:
time: 104 us; the launch traced here: 103 us
  Pallas kernels  37.1 us (36%)
  blocking collectives  34.2 us (33%)
  waiting for transfers between devices  14.2 us (14%)
  starting transfers between devices  13.3 us (13%)
  local copies, waits for them, and re-layouts  3.48 us (3%)
    all_to_all x2, blocking collectives, exchange(): lax.all_to_all(pay, 'rows', split_axis=0, concat_axis=0, tiled=True, axis...  34.2 us
    pallas_call x1, Pallas kernels, body(): pl.pallas_call(functools.partial(fold_kernel, group), out_shape=(term, te...  16.8 us
    ppermute x1, waiting for transfers between devices, body(): far = lax.ppermute(near, 'rows', across)  14 us
    all_to_all x2, starting transfers between devices, spread(): lax.all_to_all(partial_sums, 'rows', split_axis=0, concat_axis=0, tiled=T...  7.69 us
    pallas_call x1, Pallas kernels, body(): pl.pallas_call(functools.partial(first_kernel, group, parts), out_shape=(...  5.71 us
    pallas_call x1, Pallas kernels, body(): pl.pallas_call(functools.partial(middle_kernel, group), out_shape=(jax.Sh...  4.85 us
    unnamed x8, local copies, waits for them, and re-layouts  3.48 us
    pallas_call x2, Pallas kernels, summed(): pl.pallas_call(functools.partial(sum_kernel, seg), out_shape=(jax.ShapeDt...  3.42 us
  transfers between devices with their start and end apart: 4, of which 2 were waited for; matrix products, arithmetic and copies ran while one was open for 0% of the time, Pallas kernels for 19%

profile of v2, /device:TPU:0, one launch (start us, length us, event | category | flops | bytes accessed | tf_op | source)
XLA Modules:
  0.0 103.2 jit_solution(7068815809121872931)
XLA Ops:
  0.6 5.7 %level_first.1 = (f32[3,768,128]{2,1,0:T(8,128)}, f32[8,200,128]{2,1,0:T(8,128)S(1)}) custom-call(f32[3,768,128]{2,1,0:T(8,128)} %rhs.3, f32[3,768,768]{2,1,0:T(8,128)} %diag.3, f32[2,2,768,768]{3,2,1,0:T(8,128)} %tiles.2, f32[6,128]{1,0:T(8,128)} %bitcast.8, s32[2,1,2]{2,1,0:T(1,128)} %dest.3), custom_call_target="tpu_custom_call" | custom-call | flops 452984832 | bytes 9437184 | tf_op jit(solution)/shard_map/level_first/pallas_call | solution.py:330
  6.3 18.0 %all_to_all.20.got = f32[8,200,128]{2,1,0:T(8,128)S(1)} all-to-all(f32[8,200,128]{2,1,0:T(8,128)S(1)} %get-tuple-element.29), channel_id=1, replica_groups={{0,1,2,3,4,5,6,7},{8,9,10,11,12,13,14,15},{16,17,18,19,20,21,22,23},{24..., dimensions={0} | all-to-all | bytes 1638400 | tf_op jit(solution)/shard_map/all_to_all | solution.py:304
  24.4 1.7 %sum_parts.2 = (f32[16,96,128]{2,1,0:T(8,128)}, f32[8,8,128]{2,1,0:T(8,128)S(1)}) custom-call(f32[8,200,128]{2,1,0:T(8,128)S(1)} %all_to_all.20.got), custom_call_target="tpu_custom_call" | custom-call | flops 196608 | bytes 1572864 | tf_op jit(solution)/shard_map/sum_parts/pallas_call | solution.py:313
  26.1 4.1 %all-to-all-start.1 = ((f32[16,96,128]{2,1,0:T(8,128)}), f32[16,96,128]{2,1,0:T(8,128)S(1)}, u32[]{:S(2)}, u32[]{:S(2)}) async-start(f32[16,96,128]{2,1,0:T(8,128)} %get-tuple-element.31), calls=%async_computation.1 | async-start | bytes 1572864 | tf_op jit(solution)/shard_map/all_to_all | solution.py:309
  30.2 0.1 pad_add_fusion.half
  30.2 0.0 copy-start.3
  30.2 2.8 %collective-permute-start = (f32[8,8,128]{2,1,0:T(8,128)S(1)}, f32[8,8,128]{2,1,0:T(8,128)S(1)}, u32[]{:S(2)}, u32[]{:S(2)}) collective-permute-start(f32[8,8,128]{2,1,0:T(8,128)S(1)} %get-tuple-element.35.mine), channel_id=1, source_target_pairs={{0,8},{1,9},{2,10},{3,11},{4,12},{5,13},{6,14},{7,15},{8,0},{9,1},... | collective-permute-start | bytes 98312 | tf_op jit(solution)/shard_map/ppermute | solution.py:350
  33.0 16.8 %fold_levels.1 = (bf16[768,768]{1,0:T(8,128)(2,1)S(1)}, bf16[768,768]{1,0:T(8,128)(2,1)S(1)}, bf16[2,768,768]{2,1,0:T(8,128)(2,1)S(1)}, f32[768,128]{1,0:T(8,128)S(1)}, f32[1,128]{1,0:T(1,128)S(1)}) custom-call(f32[3,768,128]{2,1,0:T(8,128)} %rhs.3, f32[3,768,768]{2,1,0:T(8,128)} %diag.3, f32[2,2,768,768]{3,2,1,0:T(8,128)} %tiles.2, ...), custom_call_target="tpu_custom_call" | custom-call | flops 5435817984 | bytes 7077888 | tf_op jit(solution)/shard_map/fold_levels/pallas_call | solution.py:352
  49.8 0.0 copy-start
  49.8 1.4 %copy-done = bf16[2,768,768]{2,1,0:T(8,128)(2,1)} copy-done((bf16[2,768,768]{2,1,0:T(8,128)(2,1)}, bf16[2,768,768]{2,1,0:T(8,128)(2,1)S(1)}, u32[]{:S(2)}) %copy-start) | copy-done | bytes 2359320
  51.3 0.0 copy-start.2
  51.3 1.0 copy-done.2
  52.3 0.1 collective-permute-done.other
  52.4 0.0 all-to-all-done.1
  52.4 0.0 copy-done.3
  52.4 4.9 %level_middle.1 = (f32[8,200,128]{2,1,0:T(8,128)S(1)}, f32[768,128]{1,0:T(8,128)S(1)}) custom-call(f32[2,768,128]{2,1,0:T(8,128)S(1)} %bitcast.7, f32[768,128]{1,0:T(8,128)S(1)} %get-tuple-element.36.bias, bf16[768,768]{1,0:T(8,128)(2,1)S(1)} %get-tuple-element.37.m0_hi, bf16[768,768]{1,0:T(8,128)(2,1)} %copy-done.2, bf16[2,768,768]{2,1,0:T(8,128)(2,1)} %copy-done, ...), custom_call_target="tpu_custom_call" | custom-call | flops 301989888 | bytes 4718592 | tf_op jit(solution)/shard_map/level_middle/pallas_call | solution.py:368
  57.3 16.2 %all_to_all.21.got = f32[8,200,128]{2,1,0:T(8,128)S(1)} all-to-all(f32[8,200,128]{2,1,0:T(8,128)S(1)} %get-tuple-element.46), channel_id=1, replica_groups={{0,1,2,3,4,5,6,7},{8,9,10,11,12,13,14,15},{16,17,18,19,20,21,22,23},{24..., dimensions={0} | all-to-all | bytes 1638400 | tf_op jit(solution)/shard_map/all_to_all | solution.py:304
  73.5 1.7 %sum_parts.3 = (f32[16,96,128]{2,1,0:T(8,128)}, f32[1,128]{1,0:T(1,128)S(1)}) custom-call(f32[8,200,128]{2,1,0:T(8,128)S(1)} %all_to_all.21.got), custom_call_target="tpu_custom_call" | custom-call | flops 196608 | bytes 1572864 | tf_op jit(solution)/shard_map/sum_parts/pallas_call | solution.py:313
  75.2 3.6 %all-to-all-start.3 = ((f32[16,96,128]{2,1,0:T(8,128)}), f32[16,96,128]{2,1,0:T(8,128)S(1)}, u32[]{:S(2)}, u32[]{:S(2)}) async-start(f32[16,96,128]{2,1,0:T(8,128)} %get-tuple-element.47), calls=%async_computation.3 | async-start | bytes 1572864 | tf_op jit(solution)/shard_map/all_to_all | solution.py:309
  78.9 2.8 %collective-permute-start.1 = (f32[1,128]{1,0:T(1,128)S(1)}, f32[1,128]{1,0:T(1,128)S(1)}, u32[]{:S(2)}, u32[]{:S(2)}) collective-permute-start(f32[1,128]{1,0:T(1,128)S(1)} %get-tuple-element.51.near), channel_id=1, source_target_pairs={{0,8},{1,9},{2,10},{3,11},{4,12},{5,13},{6,14},{7,15},{8,0},{9,1},... | collective-permute-start | bytes 1544 | tf_op jit(solution)/shard_map/ppermute | solution.py:385
  81.6 3.0 %in_window.1 = (f32[3,768,128]{2,1,0:T(8,128)}, bf16[768,768]{1,0:T(8,128)(2,1)S(1)}, bf16[768,768]{1,0:T(8,128)(2,1)S(1)}, f32[768,128]{1,0:T(8,128)S(1)}) custom-call(f32[3,768,128]{2,1,0:T(8,128)} %get-tuple-element.28.sol_in, f32[768,128]{1,0:T(8,128)S(1)} %get-tuple-element.41.rest, f32[3,768,128]{2,1,0:T(8,128)} %rhs.3, ...), custom_call_target="tpu_custom_call", output_to_operand_aliasing={{0}: (0, {})} | custom-call | flops 150994944 | bytes 4718592 | tf_op jit(solution)/shard_map/in_window/pallas_call | solution.py:387
  84.7 0.0 copy-start.1
  84.7 1.0 copy-done.1
  85.7 14.0 %collective-permute-done.1.far = f32[1,128]{1,0:T(1,128)S(1)} collective-permute-done((f32[1,128]{1,0:T(1,128)S(1)}, f32[1,128]{1,0:T(1,128)S(1)}, u32[]{:S(2)}, u32[]{:S(2)}) %collective-permute-start.1) | collective-permute-done | bytes 544 | tf_op jit(solution)/shard_map/ppermute | solution.py:385
  99.7 0.0 all-to-all-done.3
  99.7 3.3 %level_last.1 = (f32[3,768,128]{2,1,0:T(8,128)}, f32[1,128]{1,0:T(1,128)}) custom-call(f32[3,768,128]{2,1,0:T(8,128)} %get-tuple-element.45.sol_in, f32[2,768,128]{2,1,0:T(8,128)S(1)} %bitcast.6, f32[768,128]{1,0:T(8,128)S(1)} %get-tuple-element.48.bias, bf16[768,768]{1,0:T(8,128)(2,1)S(1)} %get-tuple-element.49.d_hi, ...), custom_call_target="tpu_custom_call", output_to_operand_aliasing={{0}: (0, {})} | custom-call | flops 150994944 | bytes 2359296 | tf_op jit(solution)/shard_map/level_last/pallas_call | solution.py:402
Async XLA Ops:
  26.1 26.4 %all-to-all-start.1 = ((f32[16,96,128]{2,1,0:T(8,128)}), f32[16,96,128]{2,1,0:T(8,128)S(1)}, u32[]{:S(2)}, u32[]{:S(2)}) async-start(f32[16,96,128]{2,1,0:T(8,128)} %get-tuple-element.31), calls=%async_computation.1 | async-start | bytes 1572864 | tf_op jit(solution)/shard_map/all_to_all | solution.py:309
  30.2 22.2 %copy-start.3 = (s32[2,1,2]{2,1,0:T(1,128)S(1)}, s32[2,1,2]{2,1,0:T(1,128)}, u32[]{:S(2)}) copy-start(s32[2,1,2]{2,1,0:T(1,128)} %dest.3) | copy-start | bytes 52
  30.2 22.2 %collective-permute-start = (f32[8,8,128]{2,1,0:T(8,128)S(1)}, f32[8,8,128]{2,1,0:T(8,128)S(1)}, u32[]{:S(2)}, u32[]{:S(2)}) collective-permute-start(f32[8,8,128]{2,1,0:T(8,128)S(1)} %get-tuple-element.35.mine), channel_id=1, source_target_pairs={{0,8},{1,9},{2,10},{3,11},{4,12},{5,13},{6,14},{7,15},{8,0},{9,1},... | collective-permute-start | bytes 98312 | tf_op jit(solution)/shard_map/ppermute | solution.py:350
  49.8 1.4 %copy-start = (bf16[2,768,768]{2,1,0:T(8,128)(2,1)}, bf16[2,768,768]{2,1,0:T(8,128)(2,1)S(1)}, u32[]{:S(2)}) copy-start(bf16[2,768,768]{2,1,0:T(8,128)(2,1)S(1)} %get-tuple-element.39.m_lo) | copy-start | bytes 7077892
  51.3 1.0 copy-start.2
  75.2 24.5 %all-to-all-start.3 = ((f32[16,96,128]{2,1,0:T(8,128)}), f32[16,96,128]{2,1,0:T(8,128)S(1)}, u32[]{:S(2)}, u32[]{:S(2)}) async-start(f32[16,96,128]{2,1,0:T(8,128)} %get-tuple-element.47), calls=%async_computation.3 | async-start | bytes 1572864 | tf_op jit(solution)/shard_map/all_to_all | solution.py:309
  78.9 20.8 %collective-permute-start.1 = (f32[1,128]{1,0:T(1,128)S(1)}, f32[1,128]{1,0:T(1,128)S(1)}, u32[]{:S(2)}, u32[]{:S(2)}) collective-permute-start(f32[1,128]{1,0:T(1,128)S(1)} %get-tuple-element.51.near), channel_id=1, source_target_pairs={{0,8},{1,9},{2,10},{3,11},{4,12},{5,13},{6,14},{7,15},{8,0},{9,1},... | collective-permute-start | bytes 1544 | tf_op jit(solution)/shard_map/ppermute | solution.py:385
  84.7 1.0 copy-start.1

commit v3 on v2

v3 whole, which is shorter than its diff:
```python
import functools

import jax
import jax.numpy as jnp
from jax import lax
from jax.experimental import pallas as pl
from jax.experimental.pallas import tpu as pltpu
from jax.sharding import PartitionSpec as P

LANES = 128
SUB = 8
HBM = pl.BlockSpec(memory_space=pltpu.HBM)
ANY = pl.BlockSpec(memory_space=pl.ANY)
VMEM = pl.BlockSpec(memory_space=pltpu.VMEM)
SMEM = pl.BlockSpec(memory_space=pltpu.SMEM)


def split(x):
    hi = x.astype(jnp.bfloat16)
    lo = (x - hi.astype(jnp.float32)).astype(jnp.bfloat16)
    return hi, lo


def split_cols(x):
    hi, lo = split(x)
    return jnp.concatenate([hi, lo], axis=1)


def dot_terms(hi, lo, both):
    width = both.shape[1] // 2
    wide = jnp.dot(hi, both, preferred_element_type=jnp.float32)
    narrow = jnp.dot(lo, both[:, :width], preferred_element_type=jnp.float32)
    return wide[:, :width] + (wide[:, width:] + narrow)


def dot_late(hi, lo_ref, lo_copy, both):
    width = both.shape[1] // 2
    wide = jnp.dot(hi, both, preferred_element_type=jnp.float32)
    lo_copy.wait()
    narrow = jnp.dot(lo_ref[...], both[:, :width], preferred_element_type=jnp.float32)
    return wide[:, :width] + (wide[:, width:] + narrow)


def left_product(vector, matrix, rows):
    columns = vector.T
    total = None
    for r in range(rows // LANES):
        block = matrix[r * LANES : (r + 1) * LANES, :]
        term = jnp.sum(columns[:, r : r + 1] * block, axis=0, keepdims=True)
        total = term if total is None else total + term
    return total


def chunked(ref, buf, sem, parts):
    size = buf.shape[0] // parts
    copies = []
    for c in range(parts):
        at = pl.ds(c * size, size)
        copies.append(pltpu.make_async_copy(ref.at[at], buf.at[at], sem.at[c]))
    return copies


def put_slots(pay, k, seg, first, out):
    for s in range(out.shape[0] // seg):
        pay[first + s, pl.ds(k * seg, seg), :] = out[s * seg : (s + 1) * seg]


def send_rows(src, dst, first, size, sem):
    at = pl.ds(first, size)
    copy = pltpu.make_async_copy(src.at[:, at], dst.at[:, at], sem)
    copy.start()
    return copy


def first_kernel(
    group, parts, rhs, diag, tiles, weight, dest, sol, out_pay,
    pay, b_buf, d_buf, l0_buf, l1_buf, v_buf, y_buf, w_buf, i_buf, p_sem, small, d_sem, l0_sem, l1_sem, v_sem,
):
    rows = b_buf.shape[0]
    seg = rows // group
    size = rows // parts
    d_copies = chunked(diag.at[0], d_buf, d_sem, parts)
    l_copies = [
        chunked(tiles.at[0, 0], l0_buf, l0_sem, parts),
        chunked(tiles.at[0, 1], l1_buf, l1_sem, parts),
    ]
    v_copies = chunked(diag.at[2], v_buf, v_sem, parts)
    b_copy = pltpu.make_async_copy(rhs.at[0], b_buf, small.at[0])
    w_copy = pltpu.make_async_copy(weight, w_buf, small.at[2])
    i_copy = pltpu.make_async_copy(dest, i_buf, small.at[3])
    b_copy.start()
    for copies in (d_copies, *l_copies, v_copies):
        for copy in copies:
            copy.start()
    w_copy.start()
    i_copy.start()
    b_copy.wait()
    both = split_cols(b_buf[...])
    for c in range(parts):
        at = pl.ds(c * size, size)
        d_copies[c].wait()
        y_buf[at, :] = dot_terms(*split(d_buf[at, :]), both)
    y_copy = pltpu.make_async_copy(y_buf, sol.at[0], small.at[1])
    y_copy.start()
    both = split_cols(y_buf[...])
    puts = []
    for k, buf in enumerate((l0_buf, l1_buf)):
        for c in range(parts):
            l_copies[k][c].wait()
            out = dot_terms(*split(buf[pl.ds(c * size, size), :]), both)
            put_slots(pay, k, seg, c * (size // seg), out)
        puts.append(send_rows(pay, out_pay, k * seg, seg, p_sem.at[k]))
    w_copy.wait()
    i_copy.wait()
    for copy in v_copies:
        copy.wait()
    vector = left_product(w_buf[...], v_buf, rows)
    base = 2 * seg
    extra = pay.shape[1] - base
    lines = [jnp.full((1, LANES), i_buf[0, 0, k].astype(jnp.float32)) for k in range(2)]
    lines += [vector[:, r * LANES : (r + 1) * LANES] for r in range(rows // LANES)]
    if extra > len(lines):
        lines.append(jnp.zeros((extra - len(lines), LANES), jnp.float32))
    meta = jnp.concatenate(lines, axis=0)
    for s in range(group):
        pay[s, pl.ds(base, extra), :] = meta
    puts.append(send_rows(pay, out_pay, base, extra, p_sem.at[2]))
    y_copy.wait()
    for copy in puts:
        copy.wait()


def fold_out_kernel(k, diag, tiles, out_hi, out_lo, hi_buf, lo_buf, o_sem, *refs):
    fold_kernel(k, diag, tiles, hi_buf, lo_buf, *refs)
    copies = [
        pltpu.make_async_copy(hi_buf, out_hi, o_sem.at[0]),
        pltpu.make_async_copy(lo_buf, out_lo, o_sem.at[1]),
    ]
    for copy in copies:
        copy.start()
    for copy in copies:
        copy.wait()


def fold_kernel(k, diag, tiles, m_hi, m_lo, d_buf, l_buf, d_sem, l_sem):
    rows = d_buf.shape[0]
    parts = d_sem.shape[0]
    size = rows // parts
    d_copies = chunked(diag.at[1], d_buf, d_sem, parts)
    l_copies = chunked(tiles.at[1, k], l_buf, l_sem, parts)
    for copy in (*d_copies, *l_copies):
        copy.start()
    for copy in d_copies:
        copy.wait()
    both = split_cols(d_buf[...])
    for c in range(parts):
        at = pl.ds(c * size, size)
        l_copies[c].wait()
        hi, lo = split(dot_terms(*split(l_buf[at, :]), both))
        m_hi[at, :] = hi
        m_lo[at, :] = lo


def share_kernel(rhs, mine, half, share, t_buf, sem):
    rows = t_buf.shape[0]
    copy = pltpu.make_async_copy(rhs.at[2], t_buf, sem)
    copy.start()
    copy.wait()
    share[...] = left_product(mine[half[1]][2 : 2 + rows // LANES, :], t_buf, rows)


def middle_kernel(
    group, arrived, rhs, m1_hi, m1_lo, m0_hi, m0_lo, share, mine, other, dest, half,
    out_pay, out_rest, pay, rest, bias, o_hi, o_lo, v_buf, sem, v_sem, p_sem,
):
    rows = bias.shape[0]
    seg = rows // group
    count = rows // LANES
    bias_copy = pltpu.make_async_copy(rhs.at[1], bias, sem.at[2])
    bias_copy.start()
    hi_copy = pltpu.make_async_copy(m0_hi, o_hi, sem.at[0])
    lo_copy = pltpu.make_async_copy(m0_lo, o_lo, sem.at[1])
    hi_copy.start()
    lo_copy.start()
    picks = []
    for k in range(2):
        place = lax.rem(dest[1, 0, k], group)
        picks.append(pltpu.make_async_copy(mine.at[place], v_buf.at[k], v_sem.at[k]))
    for copy in picks:
        copy.start()
    bias_copy.wait()
    rest[...] = bias[...] - (arrived[0] + arrived[1])
    rest_copy = pltpu.make_async_copy(rest, out_rest, p_sem.at[3])
    rest_copy.start()
    both = split_cols(rest[...])
    part = share[...]
    puts = []
    for copy in picks:
        copy.wait()
    for k in (1, 0):
        if k == 1:
            out = dot_terms(m1_hi[...], m1_lo[...], both)
        else:
            hi_copy.wait()
            out = dot_late(o_hi[...], o_lo, lo_copy, both)
        put_slots(pay, k, seg, 0, out)
        puts.append(send_rows(pay, out_pay, k * seg, seg, p_sem.at[k]))
        same = (dest[1, 0, k] >= group) == (half[0] > 0)
        vector = jnp.where(same, v_buf[k], other[lax.rem(dest[1, 0, k], group)])
        part = part - left_product(vector[2 : 2 + count, :], out, rows)
    base = 2 * seg
    extra = pay.shape[1] - base
    lines = [jnp.full((1, LANES), dest[1, 0, k].astype(jnp.float32)) for k in range(2)]
    lines += [part, jnp.zeros((extra - 3, LANES), jnp.float32)]
    meta = jnp.concatenate(lines, axis=0)
    for s in range(group):
        pay[s, pl.ds(base, extra), :] = meta
    puts.append(send_rows(pay, out_pay, base, extra, p_sem.at[2]))
    for copy in (*puts, rest_copy):
        copy.wait()


def window_kernel(parts, sol_in, rest, diag, sol, d_hi, d_lo,
                  d_buf, y_buf, r_buf, d_sem, small, r_sem):
    rows = y_buf.shape[0]
    copies = [chunked(diag.at[1 + j], d_buf.at[j], d_sem.at[j], parts) for j in range(2)]
    r_copy = pltpu.make_async_copy(rest, r_buf, r_sem)
    for copy in (r_copy, *copies[0], *copies[1]):
        copy.start()
    r_copy.wait()
    both = split_cols(r_buf[...])
    size = rows // parts
    for c in range(parts):
        at = pl.ds(c * size, size)
        copies[0][c].wait()
        y_buf[at, :] = dot_terms(*split(d_buf[0, at, :]), both)
    y_copy = pltpu.make_async_copy(y_buf, sol.at[1], small)
    y_copy.start()
    for c in range(parts):
        at = pl.ds(c * size, size)
        copies[1][c].wait()
        hi, lo = split(d_buf[1, at, :])
        d_hi[at, :] = hi
        d_lo[at, :] = lo
    y_copy.wait()


def last_kernel(parts, sol_in, arrived, rhs, d_hi, d_lo, near, far, sol, seen, y_buf, bias, sem):
    rows = y_buf.shape[0]
    bias_copy = pltpu.make_async_copy(rhs.at[2], bias, sem.at[parts])
    bias_copy.start()
    seen[...] = near[...] + far[...]
    bias_copy.wait()
    both = split_cols(bias[...] - (arrived[0] + arrived[1]))
    size = rows // parts
    outs = []
    for c in range(parts):
        at = pl.ds(c * size, size)
        y_buf[at, :] = dot_terms(d_hi[at, :], d_lo[at, :], both)
        outs.append(pltpu.make_async_copy(y_buf.at[at], sol.at[2, at], sem.at[c]))
        outs[c].start()
    for copy in outs:
        copy.wait()


def sum_kernel(seg, got, whole, tail, out, where, sem, o_sem):
    group = got.shape[0]
    base = 2 * seg
    copies = [
        pltpu.make_async_copy(got.at[q, pl.ds(base, 2)], where.at[q], sem.at[q])
        for q in range(group)
    ]
    for copy in copies:
        copy.start()
    out[...] = jnp.zeros_like(out)
    if tail.shape[0] == 1:
        total = got[0, base + 2 : base + 3, :]
        for q in range(1, group):
            total = total + got[q, base + 2 : base + 3, :]
        tail[...] = total
    else:
        for q in range(group):
            tail[q] = got[q, base:, :]
    for q in range(group):
        copies[q].wait()
        for k in range(2):
            target = where[q, k, 0].astype(jnp.int32)
            out[target] += got[q, pl.ds(k * seg, seg), :]
    copy = pltpu.make_async_copy(out, whole, o_sem)
    copy.start()
    copy.wait()


def cost(flops, size):
    return pl.CostEstimate(flops=flops, bytes_accessed=size, transcendentals=0)


def limit(mib):
    return pltpu.CompilerParams(vmem_limit_bytes=mib << 20)


def body(rhs, diag_inv, tiles, dest, obs_weight):
    count = lax.axis_size("rows")
    group = count // 2
    levels, rows, width = rhs.shape
    seg = rows // group
    lines = rows // LANES
    extra = -(-(lines + 2) // SUB) * SUB
    parts = 2
    f32 = jnp.float32
    place = lax.axis_index("rows")
    halves = [list(range(group)), list(range(group, count))]
    across = [(i, (i + group) % count) for i in range(count)]
    half = jnp.stack([place // group, place % group]).astype(jnp.int32)

    def stay(x):
        return pltpu.with_memory_space_constraint(x, pltpu.HBM)

    block = pltpu.VMEM((rows, width), f32)
    square = pltpu.VMEM((rows, rows), f32)
    sems = pltpu.SemaphoreType.DMA((parts,))
    sol_shape = jax.ShapeDtypeStruct(rhs.shape, f32)
    term = jax.ShapeDtypeStruct((rows, rows), jnp.bfloat16)
    flat = jax.ShapeDtypeStruct((rows, width), f32)
    line = jax.ShapeDtypeStruct((1, width), f32)
    mat_flops = 2 * rows * rows * width
    mat_bytes = 4 * rows * rows

    def exchange(pay):
        return lax.all_to_all(
            pay, "rows", split_axis=0, concat_axis=0, tiled=True, axis_index_groups=halves
        )

    def spread(partial_sums):
        back = lax.all_to_all(partial_sums, "rows", split_axis=0, concat_axis=0, tiled=True)
        return back.reshape(2, rows, width)

    def summed(got, tail):
        return pl.pallas_call(
            functools.partial(sum_kernel, seg),
            out_shape=(
                pltpu.HBM((count, seg, width), f32),
                jax.ShapeDtypeStruct(tail, f32),
            ),
            in_specs=[VMEM],
            out_specs=(HBM, VMEM),
            scratch_shapes=[
                pltpu.VMEM((count, seg, width), f32),
                pltpu.SMEM((group, 2, width), f32),
                pltpu.SemaphoreType.DMA((group,)),
                pltpu.SemaphoreType.DMA,
            ],
            compiler_params=limit(6),
            cost_estimate=cost(2 * rows * width, 4 * 4 * rows * width),
            name="sum_parts",
        )(got)

    sol, pay = pl.pallas_call(
        functools.partial(first_kernel, group, parts),
        out_shape=(pltpu.HBM(rhs.shape, f32), pltpu.HBM((group, 2 * seg + extra, width), f32)),
        in_specs=[HBM, HBM, HBM, HBM, HBM],
        out_specs=(HBM, HBM),
        scratch_shapes=[
            pltpu.VMEM((group, 2 * seg + extra, width), f32),
            block, square, square, square, square, block,
            pltpu.VMEM((lines, LANES), f32), pltpu.SMEM(dest.shape, jnp.int32),
            pltpu.SemaphoreType.DMA((3,)), pltpu.SemaphoreType.DMA((4,)), sems, sems, sems, sems,
        ],
        compiler_params=limit(24),
        cost_estimate=cost(3 * mat_flops, 4 * mat_bytes),
        name="level_first",
    )(stay(rhs), stay(diag_inv), stay(tiles), stay(obs_weight.reshape(lines, LANES)), stay(dest))

    def fold(k, diag_in, tiles_in, leave):
        buffer = pltpu.VMEM((rows, rows), jnp.bfloat16)
        far_term = pltpu.HBM((rows, rows), jnp.bfloat16)
        extra_scratch = [buffer, buffer, pltpu.SemaphoreType.DMA((2,))] if leave else []
        return pl.pallas_call(
            functools.partial(fold_out_kernel if leave else fold_kernel, k),
            out_shape=(far_term, far_term) if leave else (term, term),
            in_specs=[HBM, HBM],
            out_specs=(HBM, HBM) if leave else (VMEM, VMEM),
            scratch_shapes=[*extra_scratch, square, square, sems, sems],
            compiler_params=limit(32),
            cost_estimate=cost(3 * rows * mat_flops // width, 3 * mat_bytes),
            name="fold_levels",
        )(stay(diag_in), stay(tiles_in))

    pay, diag_later, tiles_later = lax.optimization_barrier((pay, diag_inv, tiles))
    got = exchange(pay)
    m0_hi, m0_lo = fold(0, diag_later, tiles_later, True)
    got, m0_hi, m0_lo = lax.optimization_barrier((got, m0_hi, m0_lo))
    sums, mine = summed(got, (group, extra, width))
    sums, diag_later, tiles_later, rhs_later = lax.optimization_barrier(
        (sums, diag_inv, tiles, rhs)
    )
    other = lax.ppermute(mine, "rows", across)
    arrived = spread(sums)
    m1_hi, m1_lo = fold(1, diag_later, tiles_later, False)
    share = pl.pallas_call(
        share_kernel,
        out_shape=line,
        in_specs=[HBM, VMEM, SMEM],
        out_specs=VMEM,
        scratch_shapes=[block, pltpu.SemaphoreType.DMA],
        compiler_params=limit(4),
        cost_estimate=cost(2 * rows * width, 4 * rows * width),
        name="share",
    )(stay(rhs_later), mine, half)

    pay, rest = pl.pallas_call(
        functools.partial(middle_kernel, group),
        out_shape=(pltpu.HBM((group, 2 * seg + SUB, width), f32), pltpu.HBM((rows, width), f32)),
        in_specs=[VMEM, HBM, VMEM, VMEM, HBM, HBM, VMEM, HBM, VMEM, SMEM, SMEM],
        out_specs=(HBM, HBM),
        scratch_shapes=[
            pltpu.VMEM((group, 2 * seg + SUB, width), f32), block,
            block, pltpu.VMEM((rows, rows), jnp.bfloat16), pltpu.VMEM((rows, rows), jnp.bfloat16),
            pltpu.VMEM((2, extra, LANES), f32),
            pltpu.SemaphoreType.DMA((3,)), pltpu.SemaphoreType.DMA((2,)),
            pltpu.SemaphoreType.DMA((4,)),
        ],
        compiler_params=limit(16),
        cost_estimate=cost(2 * mat_flops, 2 * mat_bytes),
        name="level_middle",
    )(
        arrived, stay(rhs), m1_hi, m1_lo, stay(m0_hi), stay(m0_lo), share, stay(mine), other,
        dest, half,
    )

    pay, diag_later = lax.optimization_barrier((pay, diag_inv))
    got = exchange(pay)
    sol, d_hi, d_lo = pl.pallas_call(
        functools.partial(window_kernel, parts),
        out_shape=(sol_shape, term, term),
        in_specs=[HBM, HBM, HBM],
        out_specs=(HBM, VMEM, VMEM),
        scratch_shapes=[
            pltpu.VMEM((2, rows, rows), f32), block, block,
            pltpu.SemaphoreType.DMA((2, parts)), pltpu.SemaphoreType.DMA,
            pltpu.SemaphoreType.DMA,
        ],
        input_output_aliases={0: 0},
        compiler_params=limit(32),
        cost_estimate=cost(mat_flops, 2 * mat_bytes),
        name="in_window",
    )(sol, stay(rest), stay(diag_later))
    got, d_hi, d_lo = lax.optimization_barrier((got, d_hi, d_lo))
    sums, near = summed(got, (1, width))
    far = lax.ppermute(near, "rows", across)
    arrived = spread(sums)

    sol, seen = pl.pallas_call(
        functools.partial(last_kernel, parts),
        out_shape=(sol_shape, jax.ShapeDtypeStruct((1, width), f32)),
        in_specs=[HBM, VMEM, HBM, VMEM, VMEM, VMEM, VMEM],
        out_specs=(HBM, VMEM),
        scratch_shapes=[block, block, pltpu.SemaphoreType.DMA((parts + 1,))],
        input_output_aliases={0: 0},
        compiler_params=limit(16),
        cost_estimate=cost(mat_flops, mat_bytes),
        name="level_last",
    )(sol, arrived, stay(rhs), d_hi, d_lo, near, far)
    return sol, seen.reshape(width)


def solution(mesh):
    in_specs = (
        P(None, "rows", "parts"),
        P(None, "rows", None),
        P(None, "rows", None, None),
        P(None, "rows", None),
        P("rows"),
    )
    out_specs = (P(None, "rows", "parts"), P("parts"))
    return jax.shard_map(body, mesh=mesh, in_specs=in_specs, out_specs=out_specs, check_vma=False)
```

time: 104 us -> 104 us (level)
  blocking collectives: 34.2 us -> 0 us
  waiting for transfers between devices: 14.2 us -> 37.7 us
  starting transfers between devices: 13.3 us -> 22.9 us
  Pallas kernels: 37.1 us -> 41.8 us
  local copies, waits for them, and re-layouts: 3.48 us -> 0.01 us
    all_to_all x2 -> x0, blocking collectives: 34.2 us -> none  [exchange(): lax.all_to_all(pay, 'rows', split_axis=0, concat_axis=0, tiled=True, axis...]
    all_to_all x0 -> x2, waiting for transfers between devices: none -> 10.4 us  [exchange(): lax.all_to_all(pay, 'rows', split_axis=0, concat_axis=0, tiled=True, axis...]
    ppermute x1, waiting for transfers between devices: 0.14 us -> 9.24 us  [body(): other = lax.ppermute(mine, 'rows', across)]
    all_to_all x0 -> x2, starting transfers between devices: none -> 8.85 us  [exchange(): lax.all_to_all(pay, 'rows', split_axis=0, concat_axis=0, tiled=True, axis...]
    ppermute x1, waiting for transfers between devices: 14 us -> 18.1 us  [body(): far = lax.ppermute(near, 'rows', across)]
    pallas_call x4 -> x6, Pallas kernels: 25 us -> 28.6 us  [the longest x2 18 us: fold(): pl.pallas_call(functools.partial(fold_out_kernel if leave else fold_kerne...]
    unnamed x8 -> x4, local copies, waits for them, and re-layouts: 3.48 us -> 0.01 us
  transfers between devices with their start and end apart: 4 -> 6, of which waited for: 2 -> 4; matrix products, arithmetic and copies ran while one was open for 0% -> 0% of each run, Pallas kernels for 19% -> 23%
where the time goes in v3:
time: 104 us; the launch traced here: 103 us
  Pallas kernels  41.8 us (40%)
  waiting for transfers between devices  37.7 us (36%)
  starting transfers between devices  22.9 us (22%)
    ppermute x1, waiting for transfers between devices, body(): far = lax.ppermute(near, 'rows', across)  18.1 us
    pallas_call x2, Pallas kernels, fold(): pl.pallas_call(functools.partial(fold_out_kernel if leave else fold_kerne...  18 us
    all_to_all x2, waiting for transfers between devices, exchange(): lax.all_to_all(pay, 'rows', split_axis=0, concat_axis=0, tiled=True, axis...  10.4 us
    ppermute x1, waiting for transfers between devices, body(): other = lax.ppermute(mine, 'rows', across)  9.24 us
    all_to_all x2, starting transfers between devices, exchange(): lax.all_to_all(pay, 'rows', split_axis=0, concat_axis=0, tiled=True, axis...  8.85 us
    all_to_all x2, starting transfers between devices, spread(): lax.all_to_all(partial_sums, 'rows', split_axis=0, concat_axis=0, tiled=T...  8.52 us
    pallas_call x1, Pallas kernels, body(): pl.pallas_call(functools.partial(first_kernel, group, parts), out_shape=(...  6.35 us
    pallas_call x1, Pallas kernels, body(): pl.pallas_call(functools.partial(middle_kernel, group), out_shape=(pltpu....  5.33 us
  transfers between devices with their start and end apart: 6, of which 4 were waited for; matrix products, arithmetic and copies ran while one was open for 0% of the time, Pallas kernels for 23%

profile of v3, /device:TPU:0, one launch (start us, length us, event | category | flops | bytes accessed | tf_op | source)
XLA Modules:
  0.0 103.5 jit_solution(1669095428285774227)
XLA Ops:
  0.6 6.4 %level_first.1 = (f32[3,768,128]{2,1,0:T(8,128)}, f32[8,200,128]{2,1,0:T(8,128)}) custom-call(f32[3,768,128]{2,1,0:T(8,128)} %rhs.6, f32[3,768,768]{2,1,0:T(8,128)} %diag.4, f32[2,2,768,768]{3,2,1,0:T(8,128)} %tiles.3, f32[6,128]{1,0:T(8,128)} %bitcast.8, s32[2,1,2]{2,1,0:T(1,128)} %dest.3), custom_call_target="tpu_custom_call" | custom-call | flops 452984832 | bytes 9437184 | tf_op jit(solution)/shard_map/level_first/pallas_call | solution.py:358
  7.0 5.3 %all-to-all-start = ((f32[8,200,128]{2,1,0:T(8,128)}), f32[8,200,128]{2,1,0:T(8,128)S(1)}, u32[]{:S(2)}, u32[]{:S(2)}) async-start(f32[8,200,128]{2,1,0:T(8,128)} %get-tuple-element.36), calls=%async_computation | async-start | bytes 1638400 | tf_op jit(solution)/shard_map/all_to_all | solution.py:330
  12.3 9.7 %fold_levels.2 = (bf16[768,768]{1,0:T(8,128)(2,1)}, bf16[768,768]{1,0:T(8,128)(2,1)}) custom-call(f32[3,768,768]{2,1,0:T(8,128)} %diag.4, f32[2,2,768,768]{3,2,1,0:T(8,128)} %tiles.3), custom_call_target="tpu_custom_call" | custom-call | flops 2717908992 | bytes 7077888 | tf_op jit(solution)/shard_map/fold_levels/pallas_call | solution.py:378
  22.0 2.3 %all-to-all-done.got = f32[8,200,128]{2,1,0:T(8,128)S(1)} async-done(((f32[8,200,128]{2,1,0:T(8,128)}), f32[8,200,128]{2,1,0:T(8,128)S(1)}, u32[]{:S(2)}, u32[]{:S(2)}) %all-to-all-start) | async-done | bytes 819232 | tf_op jit(solution)/shard_map/all_to_all | solution.py:330
  24.3 1.7 %sum_parts.2 = (f32[16,96,128]{2,1,0:T(8,128)}, f32[8,8,128]{2,1,0:T(8,128)S(1)}) custom-call(f32[8,200,128]{2,1,0:T(8,128)S(1)} %all-to-all-done.got), custom_call_target="tpu_custom_call" | custom-call | flops 196608 | bytes 1572864 | tf_op jit(solution)/shard_map/sum_parts/pallas_call | solution.py:339
  26.0 0.0 copy-start
  26.0 4.9 %all-to-all-start.1 = ((f32[16,96,128]{2,1,0:T(8,128)}), f32[16,96,128]{2,1,0:T(8,128)S(1)}, u32[]{:S(2)}, u32[]{:S(2)}) async-start(f32[16,96,128]{2,1,0:T(8,128)} %get-tuple-element.43), calls=%async_computation.1 | async-start | bytes 1572864 | tf_op jit(solution)/shard_map/all_to_all | solution.py:335
  30.9 0.1 pad_add_fusion.half
  31.0 2.8 %collective-permute-start = (f32[8,8,128]{2,1,0:T(8,128)S(1)}, f32[8,8,128]{2,1,0:T(8,128)S(1)}, u32[]{:S(2)}, u32[]{:S(2)}) collective-permute-start(f32[8,8,128]{2,1,0:T(8,128)S(1)} %get-tuple-element.51.mine), channel_id=1, source_target_pairs={{0,8},{1,9},{2,10},{3,11},{4,12},{5,13},{6,14},{7,15},{8,0},{9,1},... | collective-permute-start | bytes 98312 | tf_op jit(solution)/shard_map/ppermute | solution.py:397
  33.8 8.3 %fold_levels.3 = (bf16[768,768]{1,0:T(8,128)(2,1)S(1)}, bf16[768,768]{1,0:T(8,128)(2,1)S(1)}) custom-call(f32[3,768,768]{2,1,0:T(8,128)} %diag.4, f32[2,2,768,768]{3,2,1,0:T(8,128)} %tiles.3), custom_call_target="tpu_custom_call" | custom-call | flops 2717908992 | bytes 7077888 | tf_op jit(solution)/shard_map/fold_levels/pallas_call | solution.py:378
  42.1 0.0 copy-done
  42.1 0.0 copy-start.1
  42.1 1.9 %share.1 = f32[1,128]{1,0:T(1,128)S(1)} custom-call(f32[3,768,128]{2,1,0:T(8,128)} %rhs.6, f32[8,8,128]{2,1,0:T(8,128)S(1)} %get-tuple-element.51.mine, s32[2]{0:T(128)S(1)} %pad_add_fusion.half), custom_call_target="tpu_custom_call" | custom-call | flops 196608 | bytes 393216 | tf_op jit(solution)/shard_map/share/pallas_call | solution.py:400
  44.0 9.2 %collective-permute-done.other = f32[8,8,128]{2,1,0:T(8,128)S(1)} collective-permute-done((f32[8,8,128]{2,1,0:T(8,128)S(1)}, f32[8,8,128]{2,1,0:T(8,128)S(1)}, u32[]{:S(2)}, u32[]{:S(2)}) %collective-permute-start) | collective-permute-done | bytes 32800 | tf_op jit(solution)/shard_map/ppermute | solution.py:397
  53.2 0.0 all-to-all-done.1
  53.2 0.0 copy-done.1
  53.2 5.3 %level_middle.1 = (f32[8,200,128]{2,1,0:T(8,128)}, f32[768,128]{1,0:T(8,128)}) custom-call(f32[2,768,128]{2,1,0:T(8,128)S(1)} %bitcast.6, f32[3,768,128]{2,1,0:T(8,128)} %rhs.6, bf16[768,768]{1,0:T(8,128)(2,1)S(1)} %get-tuple-element.46.m1_hi, bf16[768,768]{1,0:T(8,128)(2,1)S(1)} %get-tuple-element.47.m1_lo, bf16[768,768]{1,0:T(8,128)(2,1)} %get-tuple-element.48.m0_hi, ...), custom_call_target="tpu_custom_call" | custom-call | flops 301989888 | bytes 4718592 | tf_op jit(solution)/shard_map/level_middle/pallas_call | solution.py:411
  58.6 3.6 %all-to-all-start.2 = ((f32[8,200,128]{2,1,0:T(8,128)}), f32[8,200,128]{2,1,0:T(8,128)S(1)}, u32[]{:S(2)}, u32[]{:S(2)}) async-start(f32[8,200,128]{2,1,0:T(8,128)} %get-tuple-element.56), calls=%async_computation.2 | async-start | bytes 1638400 | tf_op jit(solution)/shard_map/all_to_all | solution.py:330
  62.1 3.9 %in_window.1 = (f32[3,768,128]{2,1,0:T(8,128)}, bf16[768,768]{1,0:T(8,128)(2,1)S(1)}, bf16[768,768]{1,0:T(8,128)(2,1)S(1)}) custom-call(f32[3,768,128]{2,1,0:T(8,128)} %get-tuple-element.34.sol_in, f32[768,128]{1,0:T(8,128)} %get-tuple-element.52.rest, f32[3,768,768]{2,1,0:T(8,128)} %diag.4), custom_call_target="tpu_custom_call", output_to_operand_aliasing={{0}: (0, {})} | custom-call | flops 150994944 | bytes 4718592 | tf_op jit(solution)/shard_map/in_window/pallas_call | solution.py:433
  66.0 8.1 %all-to-all-done.2.got = f32[8,200,128]{2,1,0:T(8,128)S(1)} async-done(((f32[8,200,128]{2,1,0:T(8,128)}), f32[8,200,128]{2,1,0:T(8,128)S(1)}, u32[]{:S(2)}, u32[]{:S(2)}) %all-to-all-start.2) | async-done | bytes 819232 | tf_op jit(solution)/shard_map/all_to_all | solution.py:330
  74.1 1.7 %sum_parts.3 = (f32[16,96,128]{2,1,0:T(8,128)}, f32[1,128]{1,0:T(1,128)S(1)}) custom-call(f32[8,200,128]{2,1,0:T(8,128)S(1)} %all-to-all-done.2.got), custom_call_target="tpu_custom_call" | custom-call | flops 196608 | bytes 1572864 | tf_op jit(solution)/shard_map/sum_parts/pallas_call | solution.py:339
  75.8 3.6 %all-to-all-start.3 = ((f32[16,96,128]{2,1,0:T(8,128)}), f32[16,96,128]{2,1,0:T(8,128)S(1)}, u32[]{:S(2)}, u32[]{:S(2)}) async-start(f32[16,96,128]{2,1,0:T(8,128)} %get-tuple-element.60), calls=%async_computation.3 | async-start | bytes 1572864 | tf_op jit(solution)/shard_map/all_to_all | solution.py:335
  79.4 2.8 %collective-permute-start.1 = (f32[1,128]{1,0:T(1,128)S(1)}, f32[1,128]{1,0:T(1,128)S(1)}, u32[]{:S(2)}, u32[]{:S(2)}) collective-permute-start(f32[1,128]{1,0:T(1,128)S(1)} %get-tuple-element.63.near), channel_id=1, source_target_pairs={{0,8},{1,9},{2,10},{3,11},{4,12},{5,13},{6,14},{7,15},{8,0},{9,1},... | collective-permute-start | bytes 1544 | tf_op jit(solution)/shard_map/ppermute | solution.py:450
  82.2 18.1 %collective-permute-done.1.far = f32[1,128]{1,0:T(1,128)S(1)} collective-permute-done((f32[1,128]{1,0:T(1,128)S(1)}, f32[1,128]{1,0:T(1,128)S(1)}, u32[]{:S(2)}, u32[]{:S(2)}) %collective-permute-start.1) | collective-permute-done | bytes 544 | tf_op jit(solution)/shard_map/ppermute | solution.py:450
  100.3 0.0 all-to-all-done.3
  100.3 3.0 %level_last.1 = (f32[3,768,128]{2,1,0:T(8,128)}, f32[1,128]{1,0:T(1,128)}) custom-call(f32[3,768,128]{2,1,0:T(8,128)} %get-tuple-element.55.sol_in, f32[2,768,128]{2,1,0:T(8,128)S(1)} %bitcast.7, f32[3,768,128]{2,1,0:T(8,128)} %rhs.6, bf16[768,768]{1,0:T(8,128)(2,1)S(1)} %get-tuple-element.61.d_hi, ...), custom_call_target="tpu_custom_call", output_to_operand_aliasing={{0}: (0, {})} | custom-call | flops 150994944 | bytes 2359296 | tf_op jit(solution)/shard_map/level_last/pallas_call | solution.py:453
Async XLA Ops:
  7.0 17.3 %all-to-all-start = ((f32[8,200,128]{2,1,0:T(8,128)}), f32[8,200,128]{2,1,0:T(8,128)S(1)}, u32[]{:S(2)}, u32[]{:S(2)}) async-start(f32[8,200,128]{2,1,0:T(8,128)} %get-tuple-element.36), calls=%async_computation | async-start | bytes 1638400 | tf_op jit(solution)/shard_map/all_to_all | solution.py:330
  26.0 16.1 %copy-start = (f32[8,8,128]{2,1,0:T(8,128)}, f32[8,8,128]{2,1,0:T(8,128)S(1)}, u32[]{:S(2)}) copy-start(f32[8,8,128]{2,1,0:T(8,128)S(1)} %get-tuple-element.51.mine) | copy-start | bytes 98308
  26.0 27.2 %all-to-all-start.1 = ((f32[16,96,128]{2,1,0:T(8,128)}), f32[16,96,128]{2,1,0:T(8,128)S(1)}, u32[]{:S(2)}, u32[]{:S(2)}) async-start(f32[16,96,128]{2,1,0:T(8,128)} %get-tuple-element.43), calls=%async_computation.1 | async-start | bytes 1572864 | tf_op jit(solution)/shard_map/all_to_all | solution.py:335
  31.0 22.2 %collective-permute-start = (f32[8,8,128]{2,1,0:T(8,128)S(1)}, f32[8,8,128]{2,1,0:T(8,128)S(1)}, u32[]{:S(2)}, u32[]{:S(2)}) collective-permute-start(f32[8,8,128]{2,1,0:T(8,128)S(1)} %get-tuple-element.51.mine), channel_id=1, source_target_pairs={{0,8},{1,9},{2,10},{3,11},{4,12},{5,13},{6,14},{7,15},{8,0},{9,1},... | collective-permute-start | bytes 98312 | tf_op jit(solution)/shard_map/ppermute | solution.py:397
  42.1 11.1 %copy-start.1 = (s32[2,1,2]{2,1,0:T(1,128)S(1)}, s32[2,1,2]{2,1,0:T(1,128)}, u32[]{:S(2)}) copy-start(s32[2,1,2]{2,1,0:T(1,128)} %dest.3) | copy-start | bytes 52
  58.6 15.5 %all-to-all-start.2 = ((f32[8,200,128]{2,1,0:T(8,128)}), f32[8,200,128]{2,1,0:T(8,128)S(1)}, u32[]{:S(2)}, u32[]{:S(2)}) async-start(f32[8,200,128]{2,1,0:T(8,128)} %get-tuple-element.56), calls=%async_computation.2 | async-start | bytes 1638400 | tf_op jit(solution)/shard_map/all_to_all | solution.py:330
  75.8 24.5 %all-to-all-start.3 = ((f32[16,96,128]{2,1,0:T(8,128)}), f32[16,96,128]{2,1,0:T(8,128)S(1)}, u32[]{:S(2)}, u32[]{:S(2)}) async-start(f32[16,96,128]{2,1,0:T(8,128)} %get-tuple-element.60), calls=%async_computation.3 | async-start | bytes 1572864 | tf_op jit(solution)/shard_map/all_to_all | solution.py:335
  79.4 20.8 %collective-permute-start.1 = (f32[1,128]{1,0:T(1,128)S(1)}, f32[1,128]{1,0:T(1,128)S(1)}, u32[]{:S(2)}, u32[]{:S(2)}) collective-permute-start(f32[1,128]{1,0:T(1,128)S(1)} %get-tuple-element.63.near), channel_id=1, source_target_pairs={{0,8},{1,9},{2,10},{3,11},{4,12},{5,13},{6,14},{7,15},{8,0},{9,1},... | collective-permute-start | bytes 1544 | tf_op jit(solution)/shard_map/ppermute | solution.py:450
